TPU v7x, 128 devices: a whole 4x4x4 slice. The times are simulated.
128 devices in a mesh: tm: 8 (over y, core), tile: 16 (over x, z).
Axes of the slice: x: 4, y: 4, z: 4, core: 2. Of those that a mesh axis runs over, the one named last changes fastest.
Arguments:
- movie: bfloat16 [32, 1024, 1024], P('tm', 'tile'), may hold values from -6 to 6
- lift_weight: float32 [24], replicated, may hold values from -4 to 4
- lift_bias: float32 [24], replicated, may hold values from -3 to 3
- depth_kernel: float32 [3, 24, 9], replicated, may hold values from -2 to 2
- mix_weight: bfloat16 [3, 24, 24], replicated, may hold values from -1.25 to 1.25
- mix_bias: float32 [3, 24], replicated, may hold values from -3 to 3
- out_weight: float32 [24], replicated, may hold values from -1.25 to 1.25
- temporal_kernel: float32 [9], replicated, may hold values from -2 to 2
- footprints: bfloat16 [256, 1024, 1024], P(None, 'tile', 'tm'), may hold values from -0.0625 to 0.0625
- slot_owner: int32 [32768, 1], P(('tm', 'tile')), may hold values from 0 to 127; in each aligned block of 256 rows (0 to 255, 256 to 511, ...) at most 4 rows name the same one
- slot_neuron: int32 [32768], P(('tm', 'tile')), may hold values from 0 to 319
Outputs:
- filtered: bfloat16 [32, 1024, 1024], P(None, 'tile', 'tm')
- traces: float32 [40960, 32], P(('tm', 'tile'))
Inputs may be any that keep to these rules, and one draw needn't show every extreme that they name: `slot_owner`: within the rows of one device (256 aligned rows), no owner is named more than 4 times.
All inputs are finite; a program needn't handle non-finite values.
Results may differ from a plain program's by a relative error of at most 0.012.
Values may be sent and summed in bfloat16 or wider, within the bound.
No kernel may reach another device: no remote copies, remote signals or barrier semaphores. Data moves between devices by JAX's collectives and lax.ppermute only.
A program may use at most 128 MiB of HBM per device.

v0:
```python
import jax
import jax.numpy as jnp
from jax import lax
from jax.sharding import Mesh
from jax.sharding import PartitionSpec as P

LAYERS = 3
NEUR_DEV = 320
TM = ("tm_0", "tm_1")
TM_TILE = ("tm_0", "tm_1", "tile")


def with_halo(block, sides, width):
    for axis, dim in sides:
        count = lax.axis_size(axis)
        forward = [(i, i + 1) for i in range(count - 1)]
        backward = [(target, source) for source, target in forward]
        low = lax.ppermute(
            lax.slice_in_dim(block, block.shape[dim] - width, None, axis=dim), axis, forward
        )
        high = lax.ppermute(lax.slice_in_dim(block, 0, width, axis=dim), axis, backward)
        block = jnp.concatenate([low, block, high], axis=dim)
    return block


def cut_along(shard, dim, count):
    lengths = shard.shape
    tiles = shard.reshape(*lengths[:dim], count, lengths[dim] // count, *lengths[dim + 1 :])
    return jnp.moveaxis(tiles, dim, 0)


def in_order(tiles, dim):
    lengths = list(tiles.shape[1:])
    lengths[dim] *= tiles.shape[0]
    return jnp.moveaxis(tiles, 0, dim).reshape(lengths)


def exchange_in_order(tiles, axes, sequence):
    lengths = [lax.axis_size(a) for a in axes]
    tiles = tiles.reshape(*lengths, *tiles.shape[1:])
    for k in sequence:
        tiles = lax.all_to_all(tiles, axes[k], split_axis=k, concat_axis=k, tiled=True)
    return tiles.reshape(-1, *tiles.shape[len(axes) :])


def exchange_by_chip(shard, groups, sequence, split_dim, concat_dim):
    count = lax.axis_size(groups[0]) * lax.axis_size(groups[1])
    tiles = cut_along(shard, split_dim, count)
    return in_order(exchange_in_order(tiles, groups, sequence), concat_dim)


def one_exchange(shard, axis, axes, splits, concats):
    sizes = [lax.axis_size(a) for a in axes]
    tiles = cut_along(shard, splits[0], sizes[0])
    tiles = jnp.moveaxis(cut_along(tiles, splits[1] + 1, sizes[1]), 0, 1)
    inside = tiles.shape[2:]
    tiles = tiles.reshape(-1, *inside)
    tiles = lax.all_to_all(tiles, axis, split_axis=0, concat_axis=0, tiled=True)
    tiles = in_order(tiles.reshape(*sizes, *inside), concats[0] + 1)
    return in_order(tiles, concats[1])


def depthwise(features, kernel):
    row_count = features.shape[2] - 2
    col_count = features.shape[3]
    padded = jnp.pad(features, ((0, 0), (0, 0), (0, 0), (1, 1)))
    summed = jnp.zeros(features.shape[:2] + (row_count, col_count), jnp.float32)
    for row_shift in range(3):
        for col_shift in range(3):
            weight_tap = kernel[:, row_shift * 3 + col_shift][None, :, None, None]
            window = padded[
                :, :, row_shift : row_shift + row_count, col_shift : col_shift + col_count
            ]
            summed = summed + weight_tap * window.astype(jnp.float32)
    return summed


def layer_update(features, kernel, mixing, offsets):
    spread = depthwise(features, kernel).astype(jnp.bfloat16)
    mixed_sum = jnp.einsum("fcrw,cd->fdrw", spread, mixing, preferred_element_type=jnp.float32)
    mixed_sum = mixed_sum + offsets[None, :, None, None]
    return features[:, :, 1:-1].astype(jnp.float32) + jnp.maximum(mixed_sum, 0.0)


def lifted(frames_in, lift_weight, lift_bias):
    return (
        lift_weight[None, :, None, None] * frames_in.astype(jnp.float32)[:, None]
        + lift_bias[None, :, None, None]
    )


def temporal(received, temporal_kernel):
    frame_count = received.shape[0]
    tap_count = temporal_kernel.shape[0]
    half_taps = tap_count // 2
    padded = jnp.pad(received.astype(jnp.float32), ((half_taps, half_taps), (0, 0), (0, 0)))
    summed = jnp.zeros(received.shape, jnp.float32)
    for tap_index in range(tap_count):
        summed = summed + temporal_kernel[tap_index] * padded[tap_index : tap_index + frame_count]
    return summed.astype(jnp.bfloat16)


def local(
    movie,
    lift_weight,
    lift_bias,
    depth_kernel,
    mix_weight,
    mix_bias,
    out_weight,
    temporal_kernel,
    footprints,
    slot_owner,
    slot_neuron,
):
    row_count = movie.shape[1]
    widened = with_halo(movie, (("tile", 1),), LAYERS)
    first_row = lax.axis_index("tile") * row_count - LAYERS
    row_index = first_row + jnp.arange(row_count + 2 * LAYERS)
    inside = (row_index >= 0) & (row_index < row_count * lax.axis_size("tile"))
    features = jnp.where(
        inside[None, None, :, None], lifted(widened, lift_weight, lift_bias), 0.0
    ).astype(jnp.bfloat16)
    for depth_step in range(LAYERS):
        updated = layer_update(
            features, depth_kernel[depth_step], mix_weight[depth_step], mix_bias[depth_step]
        )
        keeping = inside[depth_step + 1 : inside.shape[0] - depth_step - 1]
        features = jnp.where(keeping[None, None, :, None], updated, 0.0).astype(jnp.bfloat16)
    projected = jnp.sum(out_weight[None, :, None, None] * features.astype(jnp.float32), axis=1)
    denoised = (movie.astype(jnp.float32) + projected).astype(jnp.bfloat16)
    filtered = temporal(exchange_by_chip(denoised, ("tm_0", "tm_1"), (1, 0), 2, 0), temporal_kernel)
    frame_total, block_rows, block_cols = filtered.shape
    slot_total = footprints.shape[0]
    partial_value = lax.dot_general(
        footprints.reshape(slot_total, block_rows * block_cols),
        filtered.reshape(frame_total, block_rows * block_cols),
        (((1,), (1,)), ((), ())),
        preferred_element_type=jnp.float32,
    )
    tm_count = lax.axis_size(TM)
    tile_count = lax.axis_size("tile")
    device_count = tm_count * tile_count
    capacity = max(4, 2 * slot_total // device_count)
    target = slot_owner[:, 0]
    chosen = (target[:, None] == jnp.arange(device_count, dtype=jnp.int32)[None, :]).astype(
        jnp.int32
    )
    earlier = jnp.cumsum(chosen, axis=0) - chosen
    position = target * capacity + jnp.sum(earlier * chosen, axis=1)
    outgoing = (
        jnp.zeros((device_count * capacity, frame_total), jnp.float32)
        .at[position]
        .set(partial_value)
    )
    outgoing_ids = jnp.zeros((device_count * capacity,), jnp.int32).at[position].set(slot_neuron)
    arriving, arriving_ids = (
        one_exchange(
            outgoing.reshape(tm_count, tile_count, capacity, frame_total).astype(jnp.bfloat16),
            TM_TILE,
            (TM, "tile"),
            (0, 1),
            (0, 1),
        ).astype(jnp.float32),
        one_exchange(
            outgoing_ids.reshape(tm_count, tile_count, capacity),
            TM_TILE,
            (TM, "tile"),
            (0, 1),
            (0, 1),
        ),
    )
    arriving = arriving.reshape(device_count * capacity, frame_total)
    arriving_ids = arriving_ids.reshape(device_count * capacity)
    traces = jax.ops.segment_sum(arriving, arriving_ids, num_segments=NEUR_DEV)
    return (filtered, traces)


def solution(mesh):
    finer = Mesh(mesh.devices.reshape(4, 2, mesh.shape["tile"]), ("tm_0", "tm_1", "tile"))
    return jax.shard_map(
        local,
        mesh=finer,
        in_specs=(
            P(TM, "tile", None),
            P(),
            P(),
            P(),
            P(),
            P(),
            P(),
            P(),
            P(None, "tile", TM),
            P(TM_TILE, None),
            P(TM_TILE),
        ),
        out_specs=(P(None, "tile", TM), P(TM_TILE, None)),
        check_vma=False,
    )
```

profile of v0, /device:TPU:1, one launch (start us, length us, event | category | flops | bytes accessed | tf_op | source)
XLA Modules:
  0.0 263.2 jit_solution(7140517441199621192)
XLA Ops:
  0.6 0.9 fusion.83
  1.5 4.4 %collective-permute-start = (bf16[4,3,1024]{2,1,0:T(4,128)(2,1)S(1)}, bf16[4,3,1024]{2,1,0:T(4,128)(2,1)S(1)}, u32[]{:S(2)}, u32[]{:S(2)}) collective-permute-start(bf16[4,3,1024]{2,1,0:T(4,128)(2,1)S(1)} %get-tuple-element.10), channel_id=1, source_target_pairs={{0,1},{1,2},{2,3},{3,4},{4,5},{5,6},{6,7},{7,8},{8,9},{9,10},{10,1... | collective-permute-start | bytes 73736 | tf_op jit(solution)/shard_map/ppermute | solution.py:18
  5.9 1.3 collective-permute-start.1
  7.2 0.8 fusion.84
  8.1 0.8 slice_bitcast_fusion.30
  8.9 0.8 copy.74
  9.7 0.2 fusion.64
  10.2 0.7 copy.75
  10.9 1.2 maximum_convert_fusion
  12.1 6.5 %select_convert_fusion = bf16[4,24,70,1024]{3,1,2,0:T(8,128)(2,1)} fusion(f32[24]{0:T(128)} %param.13, f32[4,70,1024]{2,1,0:T(8,128)S(1)} %maximum_convert_fusion, f32[24]{0:T(128)} %param.12, pred[70]{0:T(512)(128)(4,1)S(1)} %compare_and_fusion), kind=kLoop, calls=%fused_computation.9 | loop fusion | flops 27525120 | bytes 14909702 | tf_op jit(solution)/shard_map/convert_element_type | solution.py:123
  18.6 58.5 %fusion.7 = bf16[4,24,68,1024]{3,1,2,0:T(8,128)(2,1)} fusion(f32[24]{0:T(128)S(1)} %get-tuple-element.42, pred[68]{0:T(512)(128)(4,1)S(1)} %slice.277, bf16[4,24,70,1024]{3,1,2,0:T(8,128)(2,1)} %select_convert_fusion, f32[24]{0:T(128)S(1)} %get-tuple-element.34, f32[24]{0:T(128)S(1)} %get-tuple-element.35, f32[24]{0:T(128)S(1)} %get-tuple-element.36, ...), kind=kOutput, calls=%fused_computation.17 | convolution fusion | flops 541458432 | bytes 80621056 | tf_op jit(solution)/shard_map/fcrw,cd->fdrw/dot_general | solution.py:80
  77.1 57.6 %fusion.15 = bf16[4,24,66,1024]{3,1,2,0:T(8,128)(2,1)} fusion(f32[24]{0:T(128)S(1)} %get-tuple-element.44, pred[66]{0:T(512)(128)(4,1)S(1)} %slice.276, bf16[4,24,68,1024]{3,1,2,0:T(8,128)(2,1)} %fusion.7, f32[24]{0:T(128)S(1)} %get-tuple-element.25, f32[24]{0:T(128)S(1)} %get-tuple-element.26, f32[24]{0:T(128)S(1)} %get-tuple-element.27, ...), kind=kOutput, calls=%fused_computation.25 | convolution fusion | flops 525533184 | bytes 78261760 | tf_op jit(solution)/shard_map/fcrw,cd->fdrw/dot_general | solution.py:80
  134.7 62.8 %multiply_reduce_fusion = f32[4,64,1024]{2,1,0:T(8,128)S(1)} fusion(f32[24]{0:T(128)S(1)} %get-tuple-element.43, f32[24]{0:T(128)S(1)} %copy-done.6, pred[64]{0:T(512)(128)(4,1)S(1)} %slice.275, bf16[4,24,66,1024]{3,1,2,0:T(8,128)(2,1)} %fusion.15, f32[24]{0:T(128)S(1)} %get-tuple-element.16, f32[24]{0:T(128)S(1)} %get-tuple-element.17, ...), kind=kOutput, calls=%fused_computation.34 | convolution fusion | flops 528220160 | bytes 64368640 | tf_op jit(solution)/shard_map/fcrw,cd->fdrw/dot_general | solution.py:80
  197.5 0.1 add_convert_fusion
  197.9 5.5 %all_to_all.20 = bf16[4,2,4,64,128]{4,3,2,0,1:T(8,128)(2,1)S(1)} all-to-all(bf16[4,2,4,64,128]{4,3,2,0,1:T(8,128)(2,1)S(1)} %copy.72), channel_id=1, replica_groups=mesh['tm_0'=4,'tm_1'=2,'tile'=16] {'tm_1'}, dimensions={1} | all-to-all | bytes 1048576 | tf_op jit(solution)/shard_map/all_to_all | solution.py:42
  203.5 0.8 copy.73
  204.3 4.2 %all-to-all-start.1 = ((bf16[4,2,4,64,128]{4,3,2,1,0:T(8,128)(2,1)}), bf16[4,2,4,64,128]{4,3,2,1,0:T(8,128)(2,1)S(1)}, u32[]{:S(2)}, u32[]{:S(2)}) async-start(bf16[4,2,4,64,128]{4,3,2,1,0:T(8,128)(2,1)} %copy.73), calls=%async_computation.1 | async-start | bytes 1048576 | tf_op jit(solution)/shard_map/all_to_all | solution.py:42
  208.5 0.2 fusion.66
  208.7 1.6 scatter_custom_fusion
  210.2 0.7 reshape_transpose_transpose_reshape_reshape_reshape.3
  211.0 0.7 fusion.85
  211.7 5.7 %all-to-all-done.1 = bf16[4,2,4,64,128]{4,3,2,1,0:T(8,128)(2,1)S(1)} async-done(((bf16[4,2,4,64,128]{4,3,2,1,0:T(8,128)(2,1)}), bf16[4,2,4,64,128]{4,3,2,1,0:T(8,128)(2,1)S(1)}, u32[]{:S(2)}, u32[]{:S(2)}) %all-to-all-start.1) | async-done | bytes 524320 | tf_op jit(solution)/shard_map/all_to_all | solution.py:42
  217.4 9.7 %all-to-all-start.2 = ((s32[128,1,1,4]{3,2,1,0:T(1,128)}), s32[128,1,1,4]{3,2,1,0:T(1,128)S(1)}, u32[]{:S(2)}, u32[]{:S(2)}) async-start(s32[128,1,1,4]{3,2,1,0:T(1,128)} %bitcast.65), calls=%async_computation.2 | async-start | bytes 131072 | tf_op jit(solution)/shard_map/all_to_all | solution.py:58
  227.1 0.1 bitcast_convert_fusion
  227.2 6.2 %fusion.53 = bf16[32,64,128]{2,1,0:T(8,128)(2,1)S(1)} fusion(f32[32,64,128]{2,1,0:T(8,128)S(1)} %bitcast_convert_fusion, f32[]{:T(128)} %bitcast.57, f32[]{:T(128)} %bitcast.56, f32[]{:T(128)} %bitcast.55, f32[]{:T(128)} %bitcast.54, f32[]{:T(128)} %bitcast.52, f32[]{:T(128)} %bitcast.51, f32[]{:T(128)} %bitcast.50, f32[]{:T(128)} %bitcast.49, f32[]{:T(128)} %bitcast), kind=kLoop, calls=%fused_computation.67 | loop fusion | flops 4718592 | bytes 1572900 | tf_op jit(solution)/shard_map/convert_element_type | solution.py:100
  233.5 4.9 %fusion.41 = f32[256,32]{0,1:T(8,128)S(1)} fusion(bf16[256,64,128]{2,1,0:T(8,128)(2,1)} %param.19, bf16[32,64,128]{2,1,0:T(8,128)(2,1)S(1)} %fusion.53), kind=kOutput, calls=%fused_computation.57 | convolution fusion | flops 134217728 | bytes 4751360 | tf_op jit(solution)/shard_map/dot_general | solution.py:135
  238.5 1.2 scatter_custom_fusion.1
  239.7 0.7 convert_element_type.217
  240.4 9.8 %all-to-all-start.3 = ((bf16[128,1,1,4,32]{4,3,2,1,0:T(4,128)(2,1)}), bf16[128,1,1,4,32]{4,3,2,1,0:T(4,128)(2,1)S(1)}, u32[]{:S(2)}, u32[]{:S(2)}) async-start(bf16[128,1,1,4,32]{4,3,2,1,0:T(4,128)(2,1)} %bitcast.73), calls=%async_computation.3 | async-start | bytes 262144 | tf_op jit(solution)/shard_map/all_to_all | solution.py:58
  250.3 9.8 %all-to-all-done.3 = bf16[128,1,1,4,32]{4,3,2,1,0:T(4,128)(2,1)S(1)} async-done(((bf16[128,1,1,4,32]{4,3,2,1,0:T(4,128)(2,1)}), bf16[128,1,1,4,32]{4,3,2,1,0:T(4,128)(2,1)S(1)}, u32[]{:S(2)}, u32[]{:S(2)}) %all-to-all-start.3) | async-done | bytes 32800 | tf_op jit(solution)/shard_map/all_to_all | solution.py:58
  260.0 2.4 scatter_custom_fusion.2
  262.5 0.7 copy.81
  (36 shorter events, 0.8 us)
Async XLA Ops:
  0.6 18.0 %copy-start.5 = (bf16[3,24,24]{2,1,0:T(8,128)(2,1)S(1)}, bf16[3,24,24]{2,1,0:T(8,128)(2,1)}, u32[]{:S(2)}) copy-start(bf16[3,24,24]{2,1,0:T(8,128)(2,1)} %param.15) | copy-start | bytes 10372
  1.5 9.4 %collective-permute-start = (bf16[4,3,1024]{2,1,0:T(4,128)(2,1)S(1)}, bf16[4,3,1024]{2,1,0:T(4,128)(2,1)S(1)}, u32[]{:S(2)}, u32[]{:S(2)}) collective-permute-start(bf16[4,3,1024]{2,1,0:T(4,128)(2,1)S(1)} %get-tuple-element.10), channel_id=1, source_target_pairs={{0,1},{1,2},{2,3},{3,4},{4,5},{5,6},{6,7},{7,8},{8,9},{9,10},{10,1... | collective-permute-start | bytes 73736 | tf_op jit(solution)/shard_map/ppermute | solution.py:18
  5.9 5.0 %collective-permute-start.1 = (bf16[4,3,1024]{2,1,0:T(4,128)(2,1)S(1)}, bf16[4,3,1024]{2,1,0:T(4,128)(2,1)S(1)}, u32[]{:S(2)}, u32[]{:S(2)}) collective-permute-start(bf16[4,3,1024]{2,1,0:T(4,128)(2,1)S(1)} %get-tuple-element.11), channel_id=1, source_target_pairs={{1,0},{2,1},{3,2},{4,3},{5,4},{6,5},{7,6},{8,7},{9,8},{10,9},{11,1... | collective-permute-start | bytes 73736 | tf_op jit(solution)/shard_map/ppermute | solution.py:21
  77.1 57.6 %copy-start.6 = (f32[24]{0:T(128)S(1)}, f32[24]{0:T(128)}, u32[]{:S(2)}) copy-start(f32[24]{0:T(128)} %param.17) | copy-start | bytes 292
  134.7 62.8 %copy-start = (bf16[4,64,1024]{2,1,0:T(8,128)(2,1)S(1)}, bf16[4,64,1024]{2,1,0:T(8,128)(2,1)}, u32[]{:S(2)}) copy-start(bf16[4,64,1024]{2,1,0:T(8,128)(2,1)} %param.11) | copy-start | bytes 1572868
  134.7 73.8 %copy-start.2 = (s32[128,2,128]{0,2,1:T(8,128)S(1)}, s32[128,2,128]{0,2,1:T(8,128)}, u32[]{:S(2)}) copy-start(s32[128,2,128]{0,2,1:T(8,128)} %copy.75) | copy-start | bytes 393220
  134.7 73.8 %copy-start.4 = (s32[256,1]{0,1:T(1,128)S(1)}, s32[256,1]{0,1:T(1,128)}, u32[]{:S(2)}) copy-start(s32[256,1]{0,1:T(1,128)} %param.20) | copy-start | bytes 3076
  134.7 76.2 %copy-start.3 = (f32[9]{0:T(128)S(1)}, f32[9]{0:T(128)}, u32[]{:S(2)}) copy-start(f32[9]{0:T(128)} %param.18) | copy-start | bytes 112
  204.3 13.1 %all-to-all-start.1 = ((bf16[4,2,4,64,128]{4,3,2,1,0:T(8,128)(2,1)}), bf16[4,2,4,64,128]{4,3,2,1,0:T(8,128)(2,1)S(1)}, u32[]{:S(2)}, u32[]{:S(2)}) async-start(bf16[4,2,4,64,128]{4,3,2,1,0:T(8,128)(2,1)} %copy.73), calls=%async_computation.1 | async-start | bytes 1048576 | tf_op jit(solution)/shard_map/all_to_all | solution.py:42
  217.4 23.0 %all-to-all-start.2 = ((s32[128,1,1,4]{3,2,1,0:T(1,128)}), s32[128,1,1,4]{3,2,1,0:T(1,128)S(1)}, u32[]{:S(2)}, u32[]{:S(2)}) async-start(s32[128,1,1,4]{3,2,1,0:T(1,128)} %bitcast.65), calls=%async_computation.2 | async-start | bytes 131072 | tf_op jit(solution)/shard_map/all_to_all | solution.py:58
  233.5 29.7 %copy-start.1 = (bf16[32,64,128]{2,1,0:T(8,128)(2,1)}, bf16[32,64,128]{2,1,0:T(8,128)(2,1)S(1)}, u32[]{:S(2)}) copy-start(bf16[32,64,128]{2,1,0:T(8,128)(2,1)S(1)} %fusion.53) | copy-start | bytes 1572868
  240.4 19.6 %all-to-all-start.3 = ((bf16[128,1,1,4,32]{4,3,2,1,0:T(4,128)(2,1)}), bf16[128,1,1,4,32]{4,3,2,1,0:T(4,128)(2,1)S(1)}, u32[]{:S(2)}, u32[]{:S(2)}) async-start(bf16[128,1,1,4,32]{4,3,2,1,0:T(4,128)(2,1)} %bitcast.73), calls=%async_computation.3 | async-start | bytes 262144 | tf_op jit(solution)/shard_map/all_to_all | solution.py:58
where the time goes:
time: 264 us; the launch traced here: 263 us
  matrix products  184 us (70%)
  starting transfers between devices  29.3 us (11%)
  other arithmetic  17.8 us (7%)
  waiting for transfers between devices  15.5 us (6%)
  local copies, waits for them, and re-layouts  10.5 us (4%)
  blocking collectives  5.54 us (2%)
    dot_general x3, matrix products, layer_update(): jnp.einsum('fcrw,cd->fdrw', spread, mixing, preferred_element_type=jnp.fl...  179 us
    all_to_all x2, starting transfers between devices, one_exchange(): tiles = lax.all_to_all(tiles, axis, split_axis=0, concat_axis=0, tiled=True)  19.5 us
    all_to_all x2, waiting for transfers between devices, one_exchange(): tiles = lax.all_to_all(tiles, axis, split_axis=0, concat_axis=0, tiled=True)  9.76 us
    convert_element_type x1, other arithmetic, local(): features = jnp.where(inside[None, None, :, None], lifted(widened, lift_we...  6.48 us
    convert_element_type x1, other arithmetic, temporal(): return summed.astype(jnp.bfloat16)  6.22 us
    all_to_all x1, waiting for transfers between devices, exchange_in_order(): lax.all_to_all(tiles, axes[k], split_axis=k, concat_axis=k, tiled=True)  5.74 us
    all_to_all x1, blocking collectives, exchange_in_order(): lax.all_to_all(tiles, axes[k], split_axis=k, concat_axis=k, tiled=True)  5.54 us
  transfers between devices with their start and end apart: 5, of which 2 were waited for; matrix products, arithmetic and copies ran while one was open for 8% of the time, Pallas kernels for 0%

commit v1 on v0

v1 whole, which is shorter than its diff:
```python
import functools

import jax
import jax.numpy as jnp
from jax import lax
from jax.experimental import pallas as pl
from jax.experimental.pallas import tpu as pltpu
from jax.sharding import PartitionSpec as P

C = 24
LAYERS = 3
R = 64
HALO = LAYERS
RH = R + 2 * HALO
RP = 72
W = 1024
NT = 32
CAP = 4
NEUR_DEV = 320
ID_BASE = 32
BF = jnp.bfloat16
F32 = jnp.float32
VMEM = pl.BlockSpec(memory_space=pltpu.VMEM)
SMEM = pl.BlockSpec(memory_space=pltpu.SMEM)


def mix_matrices(depth_kernel, mix_weight, mix_bias):
    k = depth_kernel.reshape(LAYERS, C, 3, 3)
    w = jnp.einsum(
        "lcyx,lcd->lydcx", k, mix_weight.astype(F32), precision=lax.Precision.HIGHEST
    )
    j = jnp.arange(8)
    shift = j[None, :] - j[:, None] + 1
    main = jnp.zeros((LAYERS, 3, C, 8, C, 8), F32)
    for dx in range(3):
        main = main + w[:, :, :, None, :, None, dx] * (shift == dx).astype(F32)[:, None, :]
    main = main.reshape(LAYERS, 3, 192, 192)
    right = (w[..., 2][:, :, :, None, :] * (j == 7).astype(F32)[:, None]).reshape(LAYERS, 3, 192, C)
    left = (w[..., 0][:, :, :, None, :] * (j == 0).astype(F32)[:, None]).reshape(LAYERS, 3, 192, C)
    b = jnp.repeat(mix_bias, 8, axis=1)
    hi = b.astype(BF).astype(F32)
    bias = jnp.stack([hi, b - hi] + [jnp.zeros_like(b)] * 14, axis=-1)
    bias = bias[:, None] * (jnp.arange(3) == 1).astype(F32)[None, :, None, None]
    return jnp.concatenate([main, right, left, bias], axis=-1).astype(BF)


def denoise_kernel(*refs, NA, UN):
    def accs(rows, count):
        return [pltpu.ACC(p)((rows, 256), F32) for p in range(2) for _ in range(count)]

    pl.run_scoped(functools.partial(to_groups, *refs), *accs(2 * RP, 1))
    pl.run_scoped(
        lambda *acc: denoise_body(*refs, *acc, NA=NA, UN=UN),
        *accs(192, NA),
    )
    pl.run_scoped(functools.partial(from_groups, *refs), *accs(2 * R, 1))


def group_tile(n, k, transposed):
    cols = lax.broadcasted_iota(jnp.int32, (256, 256), int(transposed)) + 256 * k
    at = lax.broadcasted_iota(jnp.int32, (256, 256), 1 - int(transposed))
    return (cols == 8 * (at % 128) + 2 * n + at // 128).astype(F32).astype(BF)


def to_groups(edge_ref, mv_ref, w_ref, lw_ref, lb_ref, ow_ref, out_ref, x_ref, f_ref, m_ref, *accs):
    for n in range(4):
        for k in range(4):
            tile = group_tile(n, k, False)
            for p in range(2):
                pltpu.matmul_push_rhs(tile, 0, p)
            for p in range(2):
                pltpu.matmul_acc_lhs(
                    accs[p], mv_ref[p, :, k * 256 : (k + 1) * 256], load_staged_rhs=0
                )
        for p in range(2):
            got = pltpu.matmul_pop(accs[p])
            for h in range(2):
                for jj in range(2):
                    m_ref[p, h, pl.ds(2 * n + jj, RP, stride=8), :] = got[
                        h * RP : (h + 1) * RP, jj * 128 : (jj + 1) * 128
                    ]


def from_groups(edge_ref, mv_ref, w_ref, lw_ref, lb_ref, ow_ref, out_ref, x_ref, f_ref, m_ref, *accs):
    def rows(p, n):
        parts = [
            [m_ref[p, h, pl.ds(8 * HALO + 2 * n + jj, R, stride=8), :] for jj in range(2)]
            for h in range(2)
        ]
        return jnp.concatenate([jnp.concatenate(q, axis=1) for q in parts], axis=0).astype(BF)

    for k in range(4):
        for n in range(4):
            tile = group_tile(n, k, True)
            for p in range(2):
                pltpu.matmul_push_rhs(tile, 0, p)
            for p in range(2):
                pltpu.matmul_acc_lhs(accs[p], rows(p, n), load_staged_rhs=0)
        for p in range(2):
            got = pltpu.matmul_pop(accs[p]).astype(BF)
            for h in range(2):
                for q in range(2):
                    out_ref[2 * k + q, 2 * p + h] = got[
                        h * R : (h + 1) * R, q * 128 : (q + 1) * 128
                    ]


def denoise_body(
    edge_ref, mv_ref, w_ref, lw_ref, lb_ref, ow_ref, out_ref, x_ref, f_ref, m_ref, *accs, NA, UN
):
    accs = (accs[:NA], accs[NA:])
    lanes = lax.broadcasted_iota(jnp.int32, (C, 128), 1)
    first = lanes == 0
    last = lanes == 127
    ones = (lax.broadcasted_iota(jnp.int32, (16, 256), 0) < 2).astype(F32).astype(BF)

    def movie_row(p, y):
        at = pl.multiple_of(y * 8, 8)
        return jnp.concatenate([m_ref[p, h, pl.ds(at, 8), :] for h in range(2)], axis=1)

    def put(p, y, new, slot):
        x_ref[p, y, 0:192, :] = new.astype(BF)
        for h in range(2):
            f_ref[slot, h] = new[:, h * 128 : (h + 1) * 128]
        right = []
        left = []
        for h in range(2):
            r0 = f_ref[slot, h, pl.ds(0, C, stride=8), :]
            l7 = f_ref[slot, h, pl.ds(7, C, stride=8), :]
            right.append(jnp.where(last, 0.0, pltpu.roll(r0, 127, 1)))
            left.append(jnp.where(first, 0.0, pltpu.roll(l7, 1, 1)))
        halo = jnp.concatenate([jnp.concatenate(right, 1), jnp.concatenate(left, 1)], 0)
        x_ref[p, y, 192:240, :] = halo.astype(BF)

    def lift_row(y, _):
        for p in range(2):
            m = movie_row(p, y)
            x_ref[p, y, 240:256, :] = ones
            put(p, y, jnp.concatenate([m * lw_ref[c] + lb_ref[c] for c in range(C)], axis=0), p)
        return 0

    lax.fori_loop(0, RH, lift_row, 0)

    def zero_edges():
        for side, rows in ((0, range(HALO)), (1, range(RH - HALO, RH))):

            @pl.when(edge_ref[side] == 1)
            def _():
                for p in range(2):
                    for y in rows:
                        x_ref[p, y, 0:240, :] = jnp.zeros((240, 256), BF)

    zero_edges()

    for layer in range(LAYERS):
        lo, hi = layer + 1, RH - layer - 1

        def tile(y, terms):
            for p in range(2):
                pltpu.matmul_push_rhs(x_ref[p, y], 0, p)
            for n, (dy, a) in enumerate(terms):
                for p in range(2):
                    pltpu.matmul_acc_lhs(
                        accs[p][a % NA], w_ref[layer, dy], load_staged_rhs=0 if n == 0 else None
                    )

        def finish(y, a, slot):
            for p in range(2):
                mixed = pltpu.matmul_pop(accs[p][a % NA])
                new = x_ref[p, y, 0:192, :].astype(F32) + jnp.maximum(mixed, 0.0)
                if layer < LAYERS - 1:
                    put(p, y, new, slot * 2 + p)
                else:
                    new = new.astype(BF).astype(F32)
                    total = new[0:8] * ow_ref[0]
                    for c in range(1, C):
                        total = total + new[8 * c : 8 * c + 8] * ow_ref[c]
                    total = movie_row(p, y) + total
                    for h in range(2):
                        at = pl.multiple_of(y * 8, 8)
                        m_ref[p, h, pl.ds(at, 8), :] = total[:, h * 128 : (h + 1) * 128]

        def step(y, i):
            tile(y, [(2, i - 1), (1, i), (0, i + 1)])
            finish(y - 1, i - 1, i % 2)

        tile(lo - 1, [(0, 0)])
        tile(lo, [(0, 1), (1, 0)])
        n_main = hi - lo - 2

        def body(b, _):
            for u in range(UN):
                step(lo + 1 + b * UN + u, 1 + u)
            return 0

        n_loop = n_main // UN
        lax.fori_loop(0, n_loop, body, 0)
        for u in range(n_main - n_loop * UN):
            step(lo + 1 + n_loop * UN + u, 1 + u)
        i = n_main + 1
        tile(hi - 1, [(2, i - 1), (1, i)])
        finish(hi - 2, i - 1, 0)
        tile(hi, [(2, i)])
        finish(hi - 1, i, 1)
        if layer < LAYERS - 1:
            zero_edges()


def denoise(edge, movie, mats, lift_weight, lift_bias, out_weight, NA=4, UN=8):
    return pl.pallas_call(
        functools.partial(denoise_kernel, NA=NA, UN=UN),
        out_shape=jax.ShapeDtypeStruct((8, 4, R, 128), BF),
        in_specs=[SMEM, VMEM, VMEM, SMEM, SMEM, SMEM],
        out_specs=VMEM,
        scratch_shapes=[
            pltpu.VMEM((2, RH, 256, 256), BF),
            pltpu.VMEM((4, 2, 192, 128), F32),
            pltpu.VMEM((2, 2, RP * 8, 128), F32),
        ],
        compiler_params=pltpu.CompilerParams(vmem_limit_bytes=56 * 2**20),
        name="denoise",
    )(edge, movie, mats, lift_weight, lift_bias, out_weight)


def gather_kernel(got_ref, out_ref):
    got = got_ref[...].astype(F32)
    ids = got[:, NT : NT + 1] * ID_BASE + got[:, NT + 1 : NT + 2]
    n_of = lax.broadcasted_iota(jnp.int32, (got.shape[0], NEUR_DEV), 1)
    hot = (n_of == ids.astype(jnp.int32)).astype(F32).astype(BF)
    out_ref[...] = lax.dot_general(
        hot, got_ref[:, :NT], (((0,), (0,)), ((), ())), preferred_element_type=F32
    )


def gather(got):
    return pl.pallas_call(
        gather_kernel,
        out_shape=jax.ShapeDtypeStruct((NEUR_DEV, NT), F32),
        in_specs=[VMEM],
        out_specs=VMEM,
        name="gather",
    )(got)


def temporal(received, temporal_kernel):
    frame_count = received.shape[0]
    tap_count = temporal_kernel.shape[0]
    half_taps = tap_count // 2
    padded = jnp.pad(received.astype(F32), ((half_taps, half_taps), (0, 0), (0, 0)))
    summed = jnp.zeros(received.shape, F32)
    for tap_index in range(tap_count):
        summed = summed + temporal_kernel[tap_index] * padded[tap_index : tap_index + frame_count]
    return summed.astype(BF)


def local(
    movie,
    lift_weight,
    lift_bias,
    depth_kernel,
    mix_weight,
    mix_bias,
    out_weight,
    temporal_kernel,
    footprints,
    slot_owner,
    slot_neuron,
):
    n_tile = lax.axis_size("tile")
    me = lax.axis_index("tile")
    up = [(i, i + 1) for i in range(n_tile - 1)]
    down = [(b, a) for a, b in up]
    low = lax.ppermute(movie[:, R - HALO :], "tile", up)
    high = lax.ppermute(movie[:, :HALO], "tile", down)
    pad = jnp.zeros((4, RP - RH, W), BF)
    widened = jnp.concatenate([low, movie, high, pad], axis=1)
    edge = jnp.stack([me == 0, me == n_tile - 1]).astype(jnp.int32)
    mats = mix_matrices(depth_kernel, mix_weight, mix_bias)
    denoised = denoise(edge, widened.reshape(2, 2 * RP, W), mats, lift_weight, lift_bias, out_weight)
    received = lax.all_to_all(denoised, "tm", 0, 0, tiled=True)
    filtered = temporal(received.reshape(NT, R, 128), temporal_kernel)
    slots = footprints.shape[0]
    partial = lax.dot_general(
        footprints.reshape(slots, R * 128),
        filtered.reshape(NT, R * 128),
        (((1,), (1,)), ((), ())),
        preferred_element_type=F32,
    )
    owner = slot_owner[:, 0]
    s = jnp.arange(slots)
    earlier = (owner[:, None] == owner[None, :]) & (s[None, :] < s[:, None])
    position = owner * CAP + jnp.sum(earlier, axis=1, dtype=jnp.int32)
    n_dev = lax.axis_size("tm") * n_tile
    hot = (jnp.arange(n_dev * CAP)[:, None] == position[None, :]).astype(BF)
    ids = jnp.stack([slot_neuron // ID_BASE, slot_neuron % ID_BASE], axis=1).astype(BF)
    sending = jnp.concatenate([partial.astype(BF), ids], axis=1)
    outgoing = lax.dot(hot, sending, preferred_element_type=F32).astype(BF)
    arriving = lax.all_to_all(
        outgoing.reshape(n_dev, CAP, NT + 2), ("tm", "tile"), 0, 0, tiled=True
    )
    return filtered, gather(arriving.reshape(n_dev * CAP, NT + 2))


def solution(mesh):
    return jax.shard_map(
        local,
        mesh=mesh,
        in_specs=(
            P("tm", "tile", None),
            P(),
            P(),
            P(),
            P(),
            P(),
            P(),
            P(),
            P(None, "tile", "tm"),
            P(("tm", "tile"), None),
            P(("tm", "tile")),
        ),
        out_specs=(P(None, "tile", "tm"), P(("tm", "tile"), None)),
        check_vma=False,
    )
```

time: 264 us -> 199 us (0.75)
  matrix products: 184 us -> 5.14 us
  local copies, waits for them, and re-layouts: 10.5 us -> 84.3 us
  Pallas kernels: 0 us -> 52.5 us
  starting transfers between devices: 29.3 us -> 11.7 us
  blocking collectives: 5.54 us -> 19.6 us
  waiting for transfers between devices: 15.5 us -> 8.43 us
  other arithmetic: 17.8 us -> 15 us
    dot_general x4 -> x2, matrix products: 184 us -> 5.14 us  [the longest x1 4.92 us: local(): lax.dot_general(footprints.reshape(slots, R * 128), filtered.reshape(NT,...]
    mul x3 -> x17, local copies, waits for them, and re-layouts: 0.02 us -> 72 us  [the longest x13 71.8 us: mix_matrices(): w[:, :, :, None, :, None, dx] * (shift == dx).astype(F32)[:, None, :]]
    pallas_call x0 -> x2, Pallas kernels: none -> 52.5 us  [the longest x1 50.5 us: denoise(): pl.pallas_call(functools.partial(denoise_kernel, NA=NA, UN=UN), out_shape...]
    all_to_all x3 -> x1, starting transfers between devices: 23.6 us -> 5.42 us  [local(): received = lax.all_to_all(denoised, 'tm', 0, 0, tiled=True)]
    all_to_all x1, blocking collectives: 5.54 us -> 19.6 us  [local(): lax.all_to_all(outgoing.reshape(n_dev, CAP, NT + 2), ('tm', 'tile'), 0, 0...]
    convert_element_type x6 -> x9, other arithmetic: 14.9 us -> 6.99 us  [the longest x1 6.21 us: temporal(): return summed.astype(BF)]
    all_to_all x3 -> x1, waiting for transfers between devices: 15.5 us -> 8.43 us  [local(): received = lax.all_to_all(denoised, 'tm', 0, 0, tiled=True)]
    another operation x3 -> x4, other arithmetic: 0.25 us -> 4.46 us
  transfers between devices with their start and end apart: 5 -> 3, of which waited for: 2 -> 1; matrix products, arithmetic and copies ran while one was open for 8% -> 44% of each run, Pallas kernels for 0% -> 0%
where the time goes in v1:
time: 199 us; the launch traced here: 198 us
  local copies, waits for them, and re-layouts  84.3 us (42%)
  Pallas kernels  52.5 us (26%)
  blocking collectives  19.6 us (10%)
  other arithmetic  15 us (8%)
  starting transfers between devices  11.7 us (6%)
  waiting for transfers between devices  8.43 us (4%)
  matrix products  5.14 us (3%)
    mul x13, local copies, waits for them, and re-layouts, mix_matrices(): w[:, :, :, None, :, None, dx] * (shift == dx).astype(F32)[:, None, :]  71.8 us
    pallas_call x1, Pallas kernels, denoise(): pl.pallas_call(functools.partial(denoise_kernel, NA=NA, UN=UN), out_shape...  50.5 us
    all_to_all x1, blocking collectives, local(): lax.all_to_all(outgoing.reshape(n_dev, CAP, NT + 2), ('tm', 'tile'), 0, 0...  19.6 us
    all_to_all x1, waiting for transfers between devices, local(): received = lax.all_to_all(denoised, 'tm', 0, 0, tiled=True)  8.43 us
    convert_element_type x1, other arithmetic, temporal(): return summed.astype(BF)  6.21 us
    all_to_all x1, starting transfers between devices, local(): received = lax.all_to_all(denoised, 'tm', 0, 0, tiled=True)  5.42 us
    ppermute x1, starting transfers between devices, local(): low = lax.ppermute(movie[:, R - HALO:], 'tile', up)  4.95 us
    dot_general x1, matrix products, local(): lax.dot_general(footprints.reshape(slots, R * 128), filtered.reshape(NT,...  4.92 us
  transfers between devices with their start and end apart: 3, of which 1 were waited for; matrix products, arithmetic and copies ran while one was open for 44% of the time, Pallas kernels for 0%

profile of v1, /device:TPU:1, one launch (start us, length us, event | category | flops | bytes accessed | tf_op | source)
XLA Modules:
  0.0 197.6 jit_solution(8877062851714800456)
XLA Ops:
  0.6 1.5 fusion.48
  2.2 5.0 %collective-permute-start = (bf16[4,3,1024]{2,1,0:T(4,128)(2,1)}, bf16[4,3,1024]{2,1,0:T(4,128)(2,1)}, u32[]{:S(2)}, u32[]{:S(2)}) collective-permute-start(bf16[4,3,1024]{2,1,0:T(4,128)(2,1)} %get-tuple-element.10), channel_id=1, source_target_pairs={{0,1},{1,2},{2,3},{3,4},{4,5},{5,6},{6,7},{7,8},{8,9},{9,10},{10,1... | collective-permute-start | bytes 73736 | tf_op jit(solution)/shard_map/ppermute | solution.py:273
  7.1 1.3 collective-permute-start.1
  8.5 0.8 copy.32
  10.1 8.5 %mul.185 = f32[3,3,24,8,24,8]{5,4,3,2,1,0:T(8,128)} broadcast(f32[3,3,24,24]{3,2,1,0:T(8,128)S(1)} %get-tuple-element.14), dimensions={0,1,2,4} | broadcast | bytes 1347840 | tf_op jit(solution)/shard_map/mul | solution.py:36
  18.6 13.8 %mul.186 = f32[3,3,192,192]{3,2,1,0:T(8,128)} reshape(f32[3,3,24,8,24,8]{5,4,3,2,1,0:T(8,128)} %mul.185) | data formatting | bytes 2654208 | tf_op jit(solution)/shard_map/mul | solution.py:36
  32.4 8.5 %mul.199 = f32[3,3,24,8,24,8]{5,4,3,2,1,0:T(8,128)} broadcast(f32[3,3,24,24]{3,2,1,0:T(8,128)S(1)} %get-tuple-element.13), dimensions={0,1,2,4} | broadcast | bytes 1347840 | tf_op jit(solution)/shard_map/mul | solution.py:36
  40.9 13.8 %mul.200 = f32[3,3,192,192]{3,2,1,0:T(8,128)} reshape(f32[3,3,24,8,24,8]{5,4,3,2,1,0:T(8,128)} %mul.199) | data formatting | bytes 2654208 | tf_op jit(solution)/shard_map/mul | solution.py:36
  54.7 8.5 %mul.192 = f32[3,3,24,8,24,8]{5,4,3,2,1,0:T(8,128)} broadcast(f32[3,3,24,24]{3,2,1,0:T(8,128)S(1)} %get-tuple-element.12), dimensions={0,1,2,4} | broadcast | bytes 1347840 | tf_op jit(solution)/shard_map/mul | solution.py:36
  63.2 13.8 %mul.193 = f32[3,3,192,192]{3,2,1,0:T(8,128)} reshape(f32[3,3,24,8,24,8]{5,4,3,2,1,0:T(8,128)} %mul.192) | data formatting | bytes 2654208 | tf_op jit(solution)/shard_map/mul | solution.py:36
  77.3 1.4 mul.188
  78.9 1.4 mul.195
  80.6 1.4 mul.202
  82.3 0.9 copy.34
  83.2 0.9 copy.35
  84.1 1.2 fusion.28
  85.3 0.7 stack.36
  86.0 0.7 stack.37
  86.8 0.7 stack.38
  87.5 2.4 %stack.39 = f32[3,192,16]{2,1,0:T(8,128)} concatenate(f32[3,192,1]{2,1,0:T(8,128)} %copy.34, f32[3,192,1]{2,1,0:T(8,128)} %copy.35, f32[3,192,2]{2,1,0:T(8,128)} %stack.36, f32[3,192,4]{2,1,0:T(8,128)} %stack.37, f32[3,192,8]{2,1,0:T(8,128)} %stack.38), dimensions={2} | concatenate | bytes 73728 | tf_op jit(solution)/shard_map/stack | solution.py:42
  89.9 1.1 multiply_convert_fusion
  91.1 2.2 %add_convert_fusion = bf16[3,3,192,192]{3,2,1,0:T(8,128)(2,1)S(1)} fusion(f32[3,3,192,192]{3,2,1,0:T(8,128)S(1)} %copy-done.1, f32[3,3,192,192]{3,2,1,0:T(8,128)} %mul.193, f32[3,3,192,192]{3,2,1,0:T(8,128)S(1)} %copy-done, f32[192,192]{1,0:T(8,128)} %mul.202, f32[192,192]{1,0:T(8,128)} %mul.195, f32[192,192]{1,0:T(8,128)} %mul.188), kind=kLoop, calls=%fused_computation.2 | loop fusion | flops 1990656 | bytes 5087232 | tf_op jit(solution)/shard_map/convert.6
  93.3 1.5 pad_maximum_fusion.refs_2_
  95.5 1.9 maximum_maximum_fusion
  97.3 50.5 %denoise.1 = bf16[8,4,64,128]{3,2,1,0:T(8,128)(2,1)} custom-call(s32[2]{0:T(128)} %add_convert_fusion.1.refs_0_, bf16[2,144,1024]{2,1,0:T(8,128)(2,1)} %bitcast.55, bf16[3,3,192,256]{3,2,1,0:T(8,128)(2,1)} %pad_maximum_fusion.refs_2_, f32[24]{0:T(128)} %refs_3_.1, f32[24]{0:T(128)} %refs_4_.1, f32[24]{0:T(128)} %refs_5_.1), custom_call_target="tpu_custom_call" | custom-call | tf_op jit(solution)/shard_map/denoise/pallas_call | solution.py:210
  147.8 5.4 %all-to-all-start = ((bf16[8,4,64,128]{3,2,1,0:T(8,128)(2,1)}), bf16[8,4,64,128]{3,2,1,0:T(8,128)(2,1)S(1)}, u32[]{:S(2)}, u32[]{:S(2)}) async-start(bf16[8,4,64,128]{3,2,1,0:T(8,128)(2,1)} %denoise.1), calls=%async_computation | async-start | bytes 1048576 | tf_op jit(solution)/shard_map/all_to_all | solution.py:280
  154.2 8.4 %all-to-all-done = bf16[8,4,64,128]{3,2,1,0:T(8,128)(2,1)S(1)} async-done(((bf16[8,4,64,128]{3,2,1,0:T(8,128)(2,1)}), bf16[8,4,64,128]{3,2,1,0:T(8,128)(2,1)S(1)}, u32[]{:S(2)}, u32[]{:S(2)}) %all-to-all-start) | async-done | bytes 524320 | tf_op jit(solution)/shard_map/all_to_all | solution.py:280
  162.7 6.2 %fusion.20 = bf16[32,64,128]{2,1,0:T(8,128)(2,1)S(1)} fusion(f32[32,64,128]{2,1,0:T(8,128)S(1)} %bitcast_convert_fusion, f32[]{:T(128)} %bitcast.20, f32[]{:T(128)} %bitcast.19, f32[]{:T(128)} %bitcast.18, f32[]{:T(128)} %bitcast.17, f32[]{:T(128)} %bitcast.15, f32[]{:T(128)} %bitcast.14, f32[]{:T(128)} %bitcast.13, f32[]{:T(128)} %bitcast.12, f32[]{:T(128)} %bitcast), kind=kLoop, calls=%fused_computation.24 | loop fusion | flops 4718592 | bytes 1572900 | tf_op jit(solution)/shard_map/convert_element_type | solution.py:253
  169.0 4.9 %fusion.8 = bf16[256,32]{0,1:T(8,128)(2,1)S(1)} fusion(bf16[256,64,128]{2,1,0:T(8,128)(2,1)} %param.19, bf16[32,64,128]{2,1,0:T(8,128)(2,1)S(1)} %fusion.20), kind=kOutput, calls=%fused_computation.14 | convolution fusion | flops 134225920 | bytes 4734976 | tf_op jit(solution)/shard_map/dot_general | solution.py:283
  174.3 19.6 %all_to_all.10 = bf16[128,4,34]{2,1,0:T(4,128)(2,1)} all-to-all(bf16[128,4,34]{2,1,0:T(4,128)(2,1)S(1)} %bitcast.56), channel_id=1, replica_groups=mesh['tm'=8,'tile'=16] {'tm','tile'}, dimensions={0} | all-to-all | bytes 69632 | tf_op jit(solution)/shard_map/all_to_all | solution.py:298
  193.9 2.1 %gather.1 = f32[320,32]{1,0:T(8,128)} custom-call(bf16[512,34]{1,0:T(8,128)(2,1)} %bitcast.57), custom_call_target="tpu_custom_call" | custom-call | tf_op jit(solution)/shard_map/gather/pallas_call | solution.py:236
  195.9 1.6 copy.39
  (53 shorter events, 4.0 us)
Async XLA Ops:
  2.2 93.3 %collective-permute-start = (bf16[4,3,1024]{2,1,0:T(4,128)(2,1)}, bf16[4,3,1024]{2,1,0:T(4,128)(2,1)}, u32[]{:S(2)}, u32[]{:S(2)}) collective-permute-start(bf16[4,3,1024]{2,1,0:T(4,128)(2,1)} %get-tuple-element.10), channel_id=1, source_target_pairs={{0,1},{1,2},{2,3},{3,4},{4,5},{5,6},{6,7},{7,8},{8,9},{9,10},{10,1... | collective-permute-start | bytes 73736 | tf_op jit(solution)/shard_map/ppermute | solution.py:273
  7.1 88.4 %collective-permute-start.1 = (bf16[4,3,1024]{2,1,0:T(4,128)(2,1)}, bf16[4,3,1024]{2,1,0:T(4,128)(2,1)}, u32[]{:S(2)}, u32[]{:S(2)}) collective-permute-start(bf16[4,3,1024]{2,1,0:T(4,128)(2,1)} %get-tuple-element.11), channel_id=1, source_target_pairs={{1,0},{2,1},{3,2},{4,3},{5,4},{6,5},{7,6},{8,7},{9,8},{10,9},{11,1... | collective-permute-start | bytes 73736 | tf_op jit(solution)/shard_map/ppermute | solution.py:274
  80.5 1.6 copy-start.8
  84.1 6.9 %copy-start.1 = (f32[3,3,192,192]{3,2,1,0:T(8,128)S(1)}, f32[3,3,192,192]{3,2,1,0:T(8,128)}, u32[]{:S(2)}) copy-start(f32[3,3,192,192]{3,2,1,0:T(8,128)} %mul.200) | copy-start | bytes 3981316
  85.3 5.7 %copy-start = (f32[3,3,192,192]{3,2,1,0:T(8,128)S(1)}, f32[3,3,192,192]{3,2,1,0:T(8,128)}, u32[]{:S(2)}) copy-start(f32[3,3,192,192]{3,2,1,0:T(8,128)} %mul.186) | copy-start | bytes 3981316
  91.0 2.2 %copy-start.2 = (bf16[3,3,192,24]{3,2,1,0:T(8,128)(2,1)S(1)}, bf16[3,3,192,24]{3,2,1,0:T(8,128)(2,1)}, u32[]{:S(2)}) copy-start(bf16[3,3,192,24]{3,2,1,0:T(8,128)(2,1)} %get-tuple-element.28) | copy-start | bytes 248836
  91.0 2.2 %copy-start.3 = (bf16[3,3,192,24]{3,2,1,0:T(8,128)(2,1)S(1)}, bf16[3,3,192,24]{3,2,1,0:T(8,128)(2,1)}, u32[]{:S(2)}) copy-start(bf16[3,3,192,24]{3,2,1,0:T(8,128)(2,1)} %get-tuple-element.29) | copy-start | bytes 248836
  93.2 2.3 %copy-start.4 = (bf16[4,64,1024]{2,1,0:T(8,128)(2,1)S(1)}, bf16[4,64,1024]{2,1,0:T(8,128)(2,1)}, u32[]{:S(2)}) copy-start(bf16[4,64,1024]{2,1,0:T(8,128)(2,1)} %param.11) | copy-start | bytes 1572868
  97.3 55.9 %copy-start.9 = (s32[256]{0:T(256)S(1)}, s32[256]{0:T(256)}, u32[]{:S(2)}) copy-start(s32[256]{0:T(256)} %param.21) | copy-start | bytes 3076
  97.3 55.9 %copy-start.6 = (f32[9]{0:T(128)S(1)}, f32[9]{0:T(128)}, u32[]{:S(2)}) copy-start(f32[9]{0:T(128)} %param.18) | copy-start | bytes 112
  97.3 56.6 %copy-start.7 = (s32[256,1]{0,1:T(1,128)S(1)}, s32[256,1]{0,1:T(1,128)}, u32[]{:S(2)}) copy-start(s32[256,1]{0,1:T(1,128)} %param.20) | copy-start | bytes 3076
  147.8 14.8 %all-to-all-start = ((bf16[8,4,64,128]{3,2,1,0:T(8,128)(2,1)}), bf16[8,4,64,128]{3,2,1,0:T(8,128)(2,1)S(1)}, u32[]{:S(2)}, u32[]{:S(2)}) async-start(bf16[8,4,64,128]{3,2,1,0:T(8,128)(2,1)} %denoise.1), calls=%async_computation | async-start | bytes 1048576 | tf_op jit(solution)/shard_map/all_to_all | solution.py:280
  169.0 4.9 %copy-start.5 = (bf16[32,64,128]{2,1,0:T(8,128)(2,1)}, bf16[32,64,128]{2,1,0:T(8,128)(2,1)S(1)}, u32[]{:S(2)}) copy-start(bf16[32,64,128]{2,1,0:T(8,128)(2,1)S(1)} %fusion.20) | copy-start | bytes 1572868

commit v2 on v1

--- a/solution.py
+++ b/solution.py
@@ -12,7 +12,6 @@
 R = 64
 HALO = LAYERS
 RH = R + 2 * HALO
-RP = 72
 W = 1024
 NT = 32
 CAP = 4
@@ -24,31 +23,59 @@
 SMEM = pl.BlockSpec(memory_space=pltpu.SMEM)
 
 
+def mix_kernel(dk_ref, mix_ref, bias_ref, out_ref):
+    col = lax.broadcasted_iota(jnp.int32, (C, 256), 1)
+    chan = lax.broadcasted_iota(jnp.int32, (C, 256), 0)
+    right = (col >= 192) & (col < 216)
+    left = (col >= 216) & (col < 240)
+    c_of = jnp.where(right, col - 192, jnp.where(left, col - 216, col // 8))
+    spread = ((c_of == chan) & (col < 240)).astype(F32)
+    j_in = lax.broadcasted_iota(jnp.int32, (8, 256), 1)
+    j_out = lax.broadcasted_iota(jnp.int32, (8, 256), 0)
+    right = (j_in >= 192) & (j_in < 216)
+    left = (j_in >= 216) & (j_in < 240)
+    dx_of = jnp.where(right, 8, jnp.where(left, -1, j_in % 8)) - j_out + 1
+    row = lax.broadcasted_iota(jnp.int32, (C, C), 0)
+    eye = row == lax.broadcasted_iota(jnp.int32, (C, C), 1)
+    over_rows = (((0,), (0,)), ((), ()))
+    for layer in range(LAYERS):
+        mixed = lax.dot_general(
+            mix_ref[layer].astype(F32), spread, over_rows, precision=lax.Precision.HIGHEST
+        )
+        taps = lax.dot_general(
+            dk_ref[layer], spread, over_rows, precision=lax.Precision.HIGHEST
+        )
+        bias = jnp.sum(jnp.where(eye, bias_ref[layer : layer + 1, :], 0.0), axis=1, keepdims=True)
+        high = bias.astype(BF).astype(F32)
+        bias = jnp.where(col == 240, high, jnp.where(col == 241, bias - high, 0.0))
+        for dy in range(3):
+            tap = jnp.zeros((8, 256), F32)
+            for dx in range(3):
+                tap = tap + jnp.where(dx_of == dx, taps[3 * dy + dx : 3 * dy + dx + 1, :], 0.0)
+            for d in range(0, C, 2):
+                both = [
+                    mixed[e : e + 1, :] * tap + (bias[e : e + 1, :] if dy == 1 else 0.0)
+                    for e in (d, d + 1)
+                ]
+                out_ref[layer, dy, 8 * d : 8 * d + 16, :] = jnp.concatenate(both, 0).astype(BF)
+
+
 def mix_matrices(depth_kernel, mix_weight, mix_bias):
-    k = depth_kernel.reshape(LAYERS, C, 3, 3)
-    w = jnp.einsum(
-        "lcyx,lcd->lydcx", k, mix_weight.astype(F32), precision=lax.Precision.HIGHEST
-    )
-    j = jnp.arange(8)
-    shift = j[None, :] - j[:, None] + 1
-    main = jnp.zeros((LAYERS, 3, C, 8, C, 8), F32)
-    for dx in range(3):
-        main = main + w[:, :, :, None, :, None, dx] * (shift == dx).astype(F32)[:, None, :]
-    main = main.reshape(LAYERS, 3, 192, 192)
-    right = (w[..., 2][:, :, :, None, :] * (j == 7).astype(F32)[:, None]).reshape(LAYERS, 3, 192, C)
-    left = (w[..., 0][:, :, :, None, :] * (j == 0).astype(F32)[:, None]).reshape(LAYERS, 3, 192, C)
-    b = jnp.repeat(mix_bias, 8, axis=1)
-    hi = b.astype(BF).astype(F32)
-    bias = jnp.stack([hi, b - hi] + [jnp.zeros_like(b)] * 14, axis=-1)
-    bias = bias[:, None] * (jnp.arange(3) == 1).astype(F32)[None, :, None, None]
-    return jnp.concatenate([main, right, left, bias], axis=-1).astype(BF)
+    return pl.pallas_call(
+        mix_kernel,
+        out_shape=jax.ShapeDtypeStruct((LAYERS, 3, 192, 256), BF),
+        in_specs=[VMEM, VMEM, VMEM],
+        out_specs=VMEM,
+        cost_estimate=pl.CostEstimate(flops=20_000_000, bytes_accessed=1_000_000, transcendentals=0),
+        name="mix_matrices",
+    )(depth_kernel, mix_weight, mix_bias)
 
 
 def denoise_kernel(*refs, NA, UN):
     def accs(rows, count):
         return [pltpu.ACC(p)((rows, 256), F32) for p in range(2) for _ in range(count)]
 
-    pl.run_scoped(functools.partial(to_groups, *refs), *accs(2 * RP, 1))
+    pl.run_scoped(functools.partial(to_groups, *refs), *accs(2 * R + 16, 1))
     pl.run_scoped(
         lambda *acc: denoise_body(*refs, *acc, NA=NA, UN=UN),
         *accs(192, NA),
@@ -62,26 +89,31 @@
     return (cols == 8 * (at % 128) + 2 * n + at // 128).astype(F32).astype(BF)
 
 
-def to_groups(edge_ref, mv_ref, w_ref, lw_ref, lb_ref, ow_ref, out_ref, x_ref, f_ref, m_ref, *accs):
+def to_groups(edge_ref, mv_ref, halo_ref, w_ref, lw_ref, lb_ref, ow_ref, out_ref, x_ref, f_ref, m_ref, *accs):
     for n in range(4):
         for k in range(4):
             tile = group_tile(n, k, False)
             for p in range(2):
                 pltpu.matmul_push_rhs(tile, 0, p)
             for p in range(2):
-                pltpu.matmul_acc_lhs(
-                    accs[p], mv_ref[p, :, k * 256 : (k + 1) * 256], load_staged_rhs=0
-                )
+                at = slice(k * 256, (k + 1) * 256)
+                rows = jnp.concatenate([mv_ref[p, :, at], halo_ref[p, :, at]], axis=0)
+                pltpu.matmul_acc_lhs(accs[p], rows, load_staged_rhs=0)
         for p in range(2):
             got = pltpu.matmul_pop(accs[p])
             for h in range(2):
                 for jj in range(2):
-                    m_ref[p, h, pl.ds(2 * n + jj, RP, stride=8), :] = got[
-                        h * RP : (h + 1) * RP, jj * 128 : (jj + 1) * 128
+                    cut = got[:, jj * 128 : (jj + 1) * 128]
+                    j = 2 * n + jj
+                    top = 2 * R + 2 * HALO * h
+                    m_ref[p, h, pl.ds(8 * HALO + j, R, stride=8), :] = cut[h * R : (h + 1) * R]
+                    m_ref[p, h, pl.ds(j, HALO, stride=8), :] = cut[top : top + HALO]
+                    m_ref[p, h, pl.ds(8 * (HALO + R) + j, HALO, stride=8), :] = cut[
+                        top + HALO : top + 2 * HALO
                     ]
 
 
-def from_groups(edge_ref, mv_ref, w_ref, lw_ref, lb_ref, ow_ref, out_ref, x_ref, f_ref, m_ref, *accs):
+def from_groups(edge_ref, mv_ref, halo_ref, w_ref, lw_ref, lb_ref, ow_ref, out_ref, x_ref, f_ref, m_ref, *accs):
     def rows(p, n):
         parts = [
             [m_ref[p, h, pl.ds(8 * HALO + 2 * n + jj, R, stride=8), :] for jj in range(2)]
@@ -106,7 +138,7 @@
 
 
 def denoise_body(
-    edge_ref, mv_ref, w_ref, lw_ref, lb_ref, ow_ref, out_ref, x_ref, f_ref, m_ref, *accs, NA, UN
+    edge_ref, mv_ref, halo_ref, w_ref, lw_ref, lb_ref, ow_ref, out_ref, x_ref, f_ref, m_ref, *accs, NA, UN
 ):
     accs = (accs[:NA], accs[NA:])
     lanes = lax.broadcasted_iota(jnp.int32, (C, 128), 1)
@@ -206,20 +238,113 @@
             zero_edges()
 
 
-def denoise(edge, movie, mats, lift_weight, lift_bias, out_weight, NA=4, UN=8):
+def denoise(edge, movie, halo, mats, lift_weight, lift_bias, out_weight, NA=4, UN=8):
     return pl.pallas_call(
         functools.partial(denoise_kernel, NA=NA, UN=UN),
         out_shape=jax.ShapeDtypeStruct((8, 4, R, 128), BF),
-        in_specs=[SMEM, VMEM, VMEM, SMEM, SMEM, SMEM],
+        in_specs=[SMEM, VMEM, VMEM, VMEM, SMEM, SMEM, SMEM],
         out_specs=VMEM,
         scratch_shapes=[
             pltpu.VMEM((2, RH, 256, 256), BF),
             pltpu.VMEM((4, 2, 192, 128), F32),
-            pltpu.VMEM((2, 2, RP * 8, 128), F32),
+            pltpu.VMEM((2, 2, RH * 8, 128), F32),
         ],
         compiler_params=pltpu.CompilerParams(vmem_limit_bytes=56 * 2**20),
         name="denoise",
-    )(edge, movie, mats, lift_weight, lift_bias, out_weight)
+    )(edge, movie, halo, mats, lift_weight, lift_bias, out_weight)
+
+
+def relay_kernel(foot_ref, own_row_ref, own_col_ref, id_ref, after_ref, out_ref, hot_ref, ids_ref, s_ref):
+    slots = foot_ref.shape[0]
+    own_row = own_row_ref[...]
+    own_col = own_col_ref[...]
+    before = lax.broadcasted_iota(jnp.int32, (slots, slots), 0) < lax.broadcasted_iota(
+        jnp.int32, (slots, slots), 1
+    )
+    rank = jnp.sum(((own_row == own_col) & before).astype(jnp.int32), axis=0, keepdims=True)
+    place = own_row * CAP + rank
+    hot = place == lax.broadcasted_iota(jnp.int32, hot_ref.shape, 0)
+    hot_ref[...] = hot.astype(F32).astype(BF)
+    ids = id_ref[...]
+    second = lax.broadcasted_iota(jnp.int32, (slots, 2), 1) == 1
+    ids_ref[...] = jnp.where(second, ids % ID_BASE, ids // ID_BASE).astype(F32).astype(BF)
+
+    def part(g, _):
+        r0 = pl.multiple_of(g * 16, 16)
+
+        def slot(b, _):
+            for u in range(16):
+                s = b * 16 + u
+                s_ref[pl.ds(s, 16, stride=slots), :] = foot_ref[s, pl.ds(r0, 16), :].astype(F32)
+            return 0
+
+        lax.fori_loop(0, slots // 16, slot, 0)
+        for q in range(8):
+            two = [s_ref[(2 * q + e) * slots : (2 * q + e + 1) * slots, :] for e in range(2)]
+            out_ref[g * 8 + q] = jnp.concatenate(two, axis=1).astype(BF)
+        return 0
+
+    lax.fori_loop(0, R // 16, part, 0)
+
+
+def relay(footprints, slot_owner, slot_neuron, n_dev, after):
+    slots = footprints.shape[0]
+    return pl.pallas_call(
+        relay_kernel,
+        out_shape=(
+            jax.ShapeDtypeStruct((R // 2, slots, 256), BF),
+            jax.ShapeDtypeStruct((n_dev * CAP, slots), BF),
+            jax.ShapeDtypeStruct((slots, 2), BF),
+        ),
+        in_specs=[VMEM] * 4 + [pl.BlockSpec(memory_space=pl.ANY)],
+        out_specs=(VMEM, VMEM, VMEM),
+        scratch_shapes=[pltpu.VMEM((16 * slots, 128), F32)],
+        compiler_params=pltpu.CompilerParams(vmem_limit_bytes=24 * 2**20),
+        cost_estimate=pl.CostEstimate(flops=20_000_000, bytes_accessed=12_000_000, transcendentals=0),
+        name="relay",
+    )(footprints, slot_owner.reshape(1, slots), slot_owner, slot_neuron.reshape(slots, 1), after)
+
+
+def trace_kernel(got_ref, tk_ref, foot_ref, hot_ref, ids_ref, filt_ref, send_ref, g_ref):
+    half = 4
+    for r0 in range(0, R, 16):
+        frames = [got_ref[t, r0 : r0 + 16, :].astype(F32) for t in range(NT)]
+        for t in range(NT):
+            total = None
+            for k in range(2 * half + 1):
+                u = t + k - half
+                if 0 <= u < NT:
+                    term = tk_ref[k] * frames[u]
+                    total = term if total is None else total + term
+            out = total.astype(BF)
+            filt_ref[t, r0 : r0 + 16, :] = out
+            g_ref[pl.ds(r0 * NT + t, 16, stride=NT), :] = out.astype(F32)
+    total = jnp.zeros((foot_ref.shape[1], NT), F32)
+    for q in range(R // 2):
+        two = [g_ref[(2 * q + e) * NT : (2 * q + e + 1) * NT, :] for e in range(2)]
+        rows = jnp.concatenate(two, axis=1).astype(BF)
+        total = total + lax.dot_general(
+            foot_ref[q], rows, (((1,), (1,)), ((), ())), preferred_element_type=F32
+        )
+    sending = jnp.concatenate([total.astype(BF).astype(F32), ids_ref[...].astype(F32)], axis=1)
+    send_ref[...] = jnp.dot(
+        hot_ref[...], sending.astype(BF), preferred_element_type=F32
+    ).astype(BF)
+
+
+def trace(received, temporal_kernel, foot, hot, ids):
+    return pl.pallas_call(
+        trace_kernel,
+        out_shape=(
+            jax.ShapeDtypeStruct((NT, R, 128), BF),
+            jax.ShapeDtypeStruct((hot.shape[0], NT + 2), BF),
+        ),
+        in_specs=[VMEM, SMEM, VMEM, VMEM, VMEM],
+        out_specs=(VMEM, VMEM),
+        scratch_shapes=[pltpu.VMEM((R * NT, 128), F32)],
+        compiler_params=pltpu.CompilerParams(vmem_limit_bytes=24 * 2**20),
+        name="trace",
+    )(received, temporal_kernel, foot, hot, ids)
 
 
 def gather_kernel(got_ref, out_ref):
@@ -228,29 +353,18 @@
     n_of = lax.broadcasted_iota(jnp.int32, (got.shape[0], NEUR_DEV), 1)
     hot = (n_of == ids.astype(jnp.int32)).astype(F32).astype(BF)
     out_ref[...] = lax.dot_general(
-        hot, got_ref[:, :NT], (((0,), (0,)), ((), ())), preferred_element_type=F32
+        got_ref[:, :NT], hot, (((0,), (0,)), ((), ())), preferred_element_type=F32
     )
 
 
 def gather(got):
     return pl.pallas_call(
         gather_kernel,
-        out_shape=jax.ShapeDtypeStruct((NEUR_DEV, NT), F32),
+        out_shape=jax.ShapeDtypeStruct((NT, NEUR_DEV), F32),
         in_specs=[VMEM],
         out_specs=VMEM,
         name="gather",
-    )(got)
-
-
-def temporal(received, temporal_kernel):
-    frame_count = received.shape[0]
-    tap_count = temporal_kernel.shape[0]
-    half_taps = tap_count // 2
-    padded = jnp.pad(received.astype(F32), ((half_taps, half_taps), (0, 0), (0, 0)))
-    summed = jnp.zeros(received.shape, F32)
-    for tap_index in range(tap_count):
-        summed = summed + temporal_kernel[tap_index] * padded[tap_index : tap_index + frame_count]
-    return summed.astype(BF)
+    )(got).T
 
 
 def local(
@@ -272,29 +386,17 @@
     down = [(b, a) for a, b in up]
     low = lax.ppermute(movie[:, R - HALO :], "tile", up)
     high = lax.ppermute(movie[:, :HALO], "tile", down)
-    pad = jnp.zeros((4, RP - RH, W), BF)
-    widened = jnp.concatenate([low, movie, high, pad], axis=1)
+    halo = jnp.concatenate([low, high], axis=1).reshape(2, 4 * HALO, W)
+    halo = jnp.pad(halo, ((0, 0), (0, 16 - 4 * HALO), (0, 0)))
     edge = jnp.stack([me == 0, me == n_tile - 1]).astype(jnp.int32)
     mats = mix_matrices(depth_kernel, mix_weight, mix_bias)
-    denoised = denoise(edge, widened.reshape(2, 2 * RP, W), mats, lift_weight, lift_bias, out_weight)
+    denoised = denoise(
+        edge, movie.reshape(2, 2 * R, W), halo, mats, lift_weight, lift_bias, out_weight
+    )
+    n_dev = lax.axis_size("tm") * n_tile
     received = lax.all_to_all(denoised, "tm", 0, 0, tiled=True)
-    filtered = temporal(received.reshape(NT, R, 128), temporal_kernel)
-    slots = footprints.shape[0]
-    partial = lax.dot_general(
-        footprints.reshape(slots, R * 128),
-        filtered.reshape(NT, R * 128),
-        (((1,), (1,)), ((), ())),
-        preferred_element_type=F32,
-    )
-    owner = slot_owner[:, 0]
-    s = jnp.arange(slots)
-    earlier = (owner[:, None] == owner[None, :]) & (s[None, :] < s[:, None])
-    position = owner * CAP + jnp.sum(earlier, axis=1, dtype=jnp.int32)
-    n_dev = lax.axis_size("tm") * n_tile
-    hot = (jnp.arange(n_dev * CAP)[:, None] == position[None, :]).astype(BF)
-    ids = jnp.stack([slot_neuron // ID_BASE, slot_neuron % ID_BASE], axis=1).astype(BF)
-    sending = jnp.concatenate([partial.astype(BF), ids], axis=1)
-    outgoing = lax.dot(hot, sending, preferred_element_type=F32).astype(BF)
+    foot, hot, ids = relay(footprints, slot_owner, slot_neuron, n_dev, denoised)
+    filtered, outgoing = trace(received.reshape(NT, R, 128), temporal_kernel, foot, hot, ids)
     arriving = lax.all_to_all(
         outgoing.reshape(n_dev, CAP, NT + 2), ("tm", "tile"), 0, 0, tiled=True
     )

time: 199 us -> 110 us (0.55)
  local copies, waits for them, and re-layouts: 84.3 us -> 10.6 us
  other arithmetic: 15 us -> 0.68 us
  Pallas kernels: 52.5 us -> 65 us
  waiting for transfers between devices: 8.43 us -> 0.01 us
  matrix products: 5.14 us -> 0 us
    mul x17 -> x0, local copies, waits for them, and re-layouts: 72 us -> none  [the longest x13 71.8 us: mix_matrices(): w[:, :, :, None, :, None, dx] * (shift == dx).astype(F32)[:, None, :]]
    pallas_call x1 -> x4, Pallas kernels: 2.06 us -> 14.7 us  [the longest x1 7.91 us: relay(): pl.pallas_call(relay_kernel, out_shape=(jax.ShapeDtypeStruct((R // 2, slo...]
    all_to_all x1, waiting for transfers between devices: 8.43 us -> 0.01 us  [local(): received = lax.all_to_all(denoised, 'tm', 0, 0, tiled=True)]
    unnamed x21 -> x16, local copies, waits for them, and re-layouts: 1.69 us -> 8.93 us
    convert_element_type x8 -> x0, other arithmetic: 6.38 us -> none  [the longest x1 6.21 us: temporal(): return summed.astype(BF)]
    another operation x7 -> x0, local copies, waits for them, and re-layouts: 5.42 us -> none  [the longest x4 4.61 us: mix_matrices(): bias = jnp.stack([hi, b - hi] + [jnp.zeros_like(b)] * 14, axis=-1)]
    dot_general x2 -> x0, matrix products: 5.14 us -> none  [the longest x1 4.92 us: local(): lax.dot_general(footprints.reshape(slots, R * 128), filtered.reshape(NT,...]
    another operation x4 -> x0, other arithmetic: 4.46 us -> none
  transfers between devices with their start and end apart: 3 -> 3, of which waited for: 1 -> 0; matrix products, arithmetic and copies ran while one was open for 44% -> 2% of each run, Pallas kernels for 0% -> 9%
where the time goes in v2:
time: 110 us; the launch traced here: 109 us
  Pallas kernels  65 us (59%)
  blocking collectives  20.8 us (19%)
  starting transfers between devices  11.4 us (10%)
  local copies, waits for them, and re-layouts  10.6 us (10%)
    pallas_call x1, Pallas kernels, denoise(): pl.pallas_call(functools.partial(denoise_kernel, NA=NA, UN=UN), out_shape...  50.3 us
    all_to_all x1, blocking collectives, local(): lax.all_to_all(outgoing.reshape(n_dev, CAP, NT + 2), ('tm', 'tile'), 0, 0...  20.8 us
    unnamed x16, local copies, waits for them, and re-layouts  8.93 us
    pallas_call x1, Pallas kernels, relay(): pl.pallas_call(relay_kernel, out_shape=(jax.ShapeDtypeStruct((R // 2, slo...  7.91 us
    all_to_all x1, starting transfers between devices, local(): received = lax.all_to_all(denoised, 'tm', 0, 0, tiled=True)  5.71 us
    ppermute x1, starting transfers between devices, local(): low = lax.ppermute(movie[:, R - HALO:], 'tile', up)  4.36 us
    pallas_call x1, Pallas kernels, trace(): pl.pallas_call(trace_kernel, out_shape=(jax.ShapeDtypeStruct((NT, R, 128)...  2.75 us
  transfers between devices with their start and end apart: 3, of which 0 were waited for; matrix products, arithmetic and copies ran while one was open for 2% of the time, Pallas kernels for 9%

profile of v2, /device:TPU:1, one launch (start us, length us, event | category | flops | bytes accessed | tf_op | source)
XLA Modules:
  0.0 109.2 jit_solution(3890700941993830180)
XLA Ops:
  0.6 0.0 copy-start.4
  0.6 0.0 copy-start.6
  0.6 0.9 fusion
  1.6 4.4 %collective-permute-start = (bf16[4,3,1024]{2,1,0:T(4,128)(2,1)S(1)}, bf16[4,3,1024]{2,1,0:T(4,128)(2,1)S(1)}, u32[]{:S(2)}, u32[]{:S(2)}) collective-permute-start(bf16[4,3,1024]{2,1,0:T(4,128)(2,1)S(1)} %get-tuple-element.12), channel_id=1, source_target_pairs={{0,1},{1,2},{2,3},{3,4},{4,5},{5,6},{6,7},{7,8},{8,9},{9,10},{10,1... | collective-permute-start | bytes 73736 | tf_op jit(solution)/shard_map/ppermute | solution.py:387
  5.9 1.3 %collective-permute-start.1 = (bf16[4,3,1024]{2,1,0:T(4,128)(2,1)S(1)}, bf16[4,3,1024]{2,1,0:T(4,128)(2,1)S(1)}, u32[]{:S(2)}, u32[]{:S(2)}) collective-permute-start(bf16[4,3,1024]{2,1,0:T(4,128)(2,1)S(1)} %get-tuple-element.13), channel_id=1, source_target_pairs={{1,0},{2,1},{3,2},{4,3},{5,4},{6,5},{7,6},{8,7},{9,8},{10,9},{11,1... | collective-permute-start | bytes 73736 | tf_op jit(solution)/shard_map/ppermute | solution.py:388
  7.2 0.6 add_convert_fusion.refs_0_
  7.9 1.4 %copy.15.dk_ref = f32[3,24,9]{2,1,0:T(8,128)} copy(f32[3,24,9]{1,0,2:T(4,128)} %param.14) | data formatting | bytes 5184 | tf_op args[3]
  9.3 2.1 %mix_matrices.1.refs_3_ = bf16[3,3,192,256]{3,2,1,0:T(8,128)(2,1)} custom-call(f32[3,24,9]{2,1,0:T(8,128)} %copy.15.dk_ref, bf16[3,24,24]{2,1,0:T(8,128)(2,1)} %mix_ref.1, f32[3,24]{1,0:T(4,128)} %bias_ref.1), custom_call_target="tpu_custom_call" | custom-call | flops 20000000 | bytes 1000000 | tf_op jit(solution)/shard_map/mix_matrices/pallas_call | solution.py:64
  11.4 0.0 collective-permute-done
  11.4 0.0 collective-permute-done.1
  11.5 0.0 copy-start.5
  11.5 0.6 pad.4.refs_2_
  12.2 50.3 %denoise.1.after_ref = bf16[8,4,64,128]{3,2,1,0:T(8,128)(2,1)} custom-call(s32[2]{0:T(128)} %add_convert_fusion.refs_0_, bf16[2,128,1024]{2,1,0:T(8,128)(2,1)} %bitcast.12, bf16[2,16,1024]{2,1,0:T(8,128)(2,1)} %pad.4.refs_2_, bf16[3,3,192,256]{3,2,1,0:T(8,128)(2,1)} %mix_matrices.1.refs_3_, f32[24]{0:T(128)} %refs_4_.1, f32[24]{0:T(128)} %refs_5_.1, f32[24]{0:T(128)} %refs_6_.1), custom_call_target="tpu_custom_call" | custom-call | tf_op jit(solution)/shard_map/denoise/pallas_call | solution.py:242
  62.4 5.7 %all-to-all-start = ((bf16[8,4,64,128]{3,2,1,0:T(8,128)(2,1)}), bf16[8,4,64,128]{3,2,1,0:T(8,128)(2,1)S(1)}, u32[]{:S(2)}, u32[]{:S(2)}) async-start(bf16[8,4,64,128]{3,2,1,0:T(8,128)(2,1)} %denoise.1.after_ref), calls=%async_computation | async-start | bytes 1048576 | tf_op jit(solution)/shard_map/all_to_all | solution.py:397
  68.1 0.0 copy-done.4
  68.1 0.1 copy.16.own_col_ref
  68.3 0.0 copy-done.6
  68.3 0.1 copy.17.id_ref
  68.4 0.0 copy-start
  68.4 1.0 copy-done
  69.5 0.0 copy-start.1
  69.5 2.2 %copy-done.1 = bf16[256,64,128]{2,1,0:T(8,128)(2,1)S(1)} copy-done((bf16[256,64,128]{2,1,0:T(8,128)(2,1)S(1)}, bf16[256,64,128]{2,1,0:T(8,128)(2,1)}, u32[]{:S(2)}) %copy-start.1) | copy-done | bytes 4194328
  71.7 7.9 %relay.1 = (bf16[32,256,256]{2,1,0:T(8,128)(2,1)S(1)}, bf16[512,256]{1,0:T(8,128)(2,1)S(1)}, bf16[256,2]{1,0:T(8,128)(2,1)S(1)}) custom-call(bf16[256,64,128]{2,1,0:T(8,128)(2,1)S(1)} %copy-done.1, s32[1,256]{1,0:T(1,128)S(1)} %bitcast.11, s32[256,1]{1,0:T(8,128)S(1)} %copy.16.own_col_ref, s32[256,1]{1,0:T(8,128)S(1)} %copy.17.id_ref, ...), custom_call_target="tpu_custom_call" | custom-call | flops 20000000 | bytes 12000000 | tf_op jit(solution)/shard_map/relay/pallas_call | solution.py:292
  79.6 0.0 copy-start.2
  79.6 1.9 %copy-done.2 = bf16[32,256,256]{2,1,0:T(8,128)(2,1)} copy-done((bf16[32,256,256]{2,1,0:T(8,128)(2,1)}, bf16[32,256,256]{2,1,0:T(8,128)(2,1)S(1)}, u32[]{:S(2)}) %copy-start.2) | copy-done | bytes 4194328
  81.5 0.0 all-to-all-done
  81.5 0.0 copy-done.5
  81.5 0.0 copy-start.3
  81.5 2.2 %copy-done.3 = bf16[32,256,256]{2,1,0:T(8,128)(2,1)S(1)} copy-done((bf16[32,256,256]{2,1,0:T(8,128)(2,1)S(1)}, bf16[32,256,256]{2,1,0:T(8,128)(2,1)}, u32[]{:S(2)}) %copy-start.3) | copy-done | bytes 4194328
  83.7 2.7 %trace.1 = (bf16[32,64,128]{2,1,0:T(8,128)(2,1)}, bf16[512,34]{1,0:T(8,128)(2,1)S(1)}) custom-call(bf16[32,64,128]{2,1,0:T(8,128)(2,1)S(1)} %bitcast.9, f32[9]{0:T(128)S(1)} %copy-done.5, bf16[32,256,256]{2,1,0:T(8,128)(2,1)S(1)} %copy-done.3, bf16[512,256]{1,0:T(8,128)(2,1)S(1)} %get-tuple-element.8.hot_ref, bf16[256,2]{1,0:T(8,128)(2,1)S(1)} %get-tuple-element.9.ids_ref), custom_call_target="tpu_custom_call" | custom-call | tf_op jit(solution)/shard_map/trace/pallas_call | solution.py:336
  86.5 20.8 %all_to_all.10 = bf16[128,4,34]{2,1,0:T(4,128)(2,1)} all-to-all(bf16[128,4,34]{2,1,0:T(4,128)(2,1)S(1)} %bitcast.10), channel_id=1, replica_groups=mesh['tm'=8,'tile'=16] {'tm','tile'}, dimensions={0} | all-to-all | bytes 69632 | tf_op jit(solution)/shard_map/all_to_all | solution.py:400
  107.3 1.9 %gather.1 = f32[32,320]{1,0:T(8,128)} custom-call(bf16[512,34]{1,0:T(8,128)(2,1)} %bitcast.13), custom_call_target="tpu_custom_call" | custom-call | tf_op jit(solution)/shard_map/gather/pallas_call | solution.py:361
  (2 shorter events, 0.1 us)
Async XLA Ops:
  0.6 67.5 %copy-start.4 = (s32[256,1]{0,1:T(1,128)S(1)}, s32[256,1]{0,1:T(1,128)}, u32[]{:S(2)}) copy-start(s32[256,1]{0,1:T(1,128)} %param.20) | copy-start | bytes 3076
  0.6 67.6 %copy-start.6 = (s32[256]{0:T(256)S(1)}, s32[256]{0:T(256)}, u32[]{:S(2)}) copy-start(s32[256]{0:T(256)} %param.21) | copy-start | bytes 3076
  1.6 9.9 %collective-permute-start = (bf16[4,3,1024]{2,1,0:T(4,128)(2,1)S(1)}, bf16[4,3,1024]{2,1,0:T(4,128)(2,1)S(1)}, u32[]{:S(2)}, u32[]{:S(2)}) collective-permute-start(bf16[4,3,1024]{2,1,0:T(4,128)(2,1)S(1)} %get-tuple-element.12), channel_id=1, source_target_pairs={{0,1},{1,2},{2,3},{3,4},{4,5},{5,6},{6,7},{7,8},{8,9},{9,10},{10,1... | collective-permute-start | bytes 73736 | tf_op jit(solution)/shard_map/ppermute | solution.py:387
  5.9 5.5 %collective-permute-start.1 = (bf16[4,3,1024]{2,1,0:T(4,128)(2,1)S(1)}, bf16[4,3,1024]{2,1,0:T(4,128)(2,1)S(1)}, u32[]{:S(2)}, u32[]{:S(2)}) collective-permute-start(bf16[4,3,1024]{2,1,0:T(4,128)(2,1)S(1)} %get-tuple-element.13), channel_id=1, source_target_pairs={{1,0},{2,1},{3,2},{4,3},{5,4},{6,5},{7,6},{8,7},{9,8},{10,9},{11,1... | collective-permute-start | bytes 73736 | tf_op jit(solution)/shard_map/ppermute | solution.py:388
  11.5 70.0 %copy-start.5 = (f32[9]{0:T(128)S(1)}, f32[9]{0:T(128)}, u32[]{:S(2)}) copy-start(f32[9]{0:T(128)} %tk_ref.1) | copy-start | bytes 112
  62.4 19.1 %all-to-all-start = ((bf16[8,4,64,128]{3,2,1,0:T(8,128)(2,1)}), bf16[8,4,64,128]{3,2,1,0:T(8,128)(2,1)S(1)}, u32[]{:S(2)}, u32[]{:S(2)}) async-start(bf16[8,4,64,128]{3,2,1,0:T(8,128)(2,1)} %denoise.1.after_ref), calls=%async_computation | async-start | bytes 1048576 | tf_op jit(solution)/shard_map/all_to_all | solution.py:397
  68.4 1.0 copy-start
  69.5 2.2 %copy-start.1 = (bf16[256,64,128]{2,1,0:T(8,128)(2,1)S(1)}, bf16[256,64,128]{2,1,0:T(8,128)(2,1)}, u32[]{:S(2)}) copy-start(bf16[256,64,128]{2,1,0:T(8,128)(2,1)} %foot_ref.1) | copy-start | bytes 12582916
  79.6 1.9 %copy-start.2 = (bf16[32,256,256]{2,1,0:T(8,128)(2,1)}, bf16[32,256,256]{2,1,0:T(8,128)(2,1)S(1)}, u32[]{:S(2)}) copy-start(bf16[32,256,256]{2,1,0:T(8,128)(2,1)S(1)} %get-tuple-element.7.foot_ref) | copy-start | bytes 12582916
  81.5 2.2 %copy-start.3 = (bf16[32,256,256]{2,1,0:T(8,128)(2,1)S(1)}, bf16[32,256,256]{2,1,0:T(8,128)(2,1)}, u32[]{:S(2)}) copy-start(bf16[32,256,256]{2,1,0:T(8,128)(2,1)} %copy-done.2) | copy-start | bytes 12582916

commit v3 on v2

--- a/solution.py
+++ b/solution.py
@@ -12,6 +12,8 @@
 R = 64
 HALO = LAYERS
 RH = R + 2 * HALO
+RP = 72
+STEP = 14
 W = 1024
 NT = 32
 CAP = 4
@@ -20,10 +22,11 @@
 BF = jnp.bfloat16
 F32 = jnp.float32
 VMEM = pl.BlockSpec(memory_space=pltpu.VMEM)
+HBM = pl.BlockSpec(memory_space=pltpu.HBM)
 SMEM = pl.BlockSpec(memory_space=pltpu.SMEM)
 
 
-def mix_kernel(dk_ref, mix_ref, bias_ref, out_ref):
+def mix_kernel(dk_ref, mix_ref, bias_ref, lw_ref, lb_ref, out_ref, lift_ref, b_ref):
     col = lax.broadcasted_iota(jnp.int32, (C, 256), 1)
     chan = lax.broadcasted_iota(jnp.int32, (C, 256), 0)
     right = (col >= 192) & (col < 216)
@@ -38,13 +41,11 @@
     row = lax.broadcasted_iota(jnp.int32, (C, C), 0)
     eye = row == lax.broadcasted_iota(jnp.int32, (C, C), 1)
     over_rows = (((0,), (0,)), ((), ()))
-    for layer in range(LAYERS):
+    for layer in range(1, LAYERS):
         mixed = lax.dot_general(
             mix_ref[layer].astype(F32), spread, over_rows, precision=lax.Precision.HIGHEST
         )
-        taps = lax.dot_general(
-            dk_ref[layer], spread, over_rows, precision=lax.Precision.HIGHEST
-        )
+        taps = jnp.dot(dk_ref[:, layer, :], spread, precision=lax.Precision.HIGHEST)
         bias = jnp.sum(jnp.where(eye, bias_ref[layer : layer + 1, :], 0.0), axis=1, keepdims=True)
         high = bias.astype(BF).astype(F32)
         bias = jnp.where(col == 240, high, jnp.where(col == 241, bias - high, 0.0))
@@ -57,18 +58,65 @@
                     mixed[e : e + 1, :] * tap + (bias[e : e + 1, :] if dy == 1 else 0.0)
                     for e in (d, d + 1)
                 ]
-                out_ref[layer, dy, 8 * d : 8 * d + 16, :] = jnp.concatenate(both, 0).astype(BF)
-
-
-def mix_matrices(depth_kernel, mix_weight, mix_bias):
+                out_ref[layer - 1, dy, 8 * d : 8 * d + 16, :] = jnp.concatenate(both, 0).astype(BF)
+
+    def column(row_value):
+        return jnp.sum(jnp.where(eye, row_value, 0.0), axis=1, keepdims=True)
+
+    first = mix_ref[0].astype(F32)
+    by_weight, by_bias = (
+        lax.dot_general(
+            first,
+            dk_ref[:, 0, :] * ref[...],
+            (((0,), (1,)), ((), ())),
+            precision=lax.Precision.HIGHEST,
+        )
+        for ref in (lw_ref, lb_ref)
+    )
+    bias = column(bias_ref[0:1, :]) + jnp.sum(by_bias, axis=1, keepdims=True)
+    high = bias.astype(BF).astype(F32)
+    bias = jnp.where(col == 29, high, jnp.where(col == 30, bias - high, 0.0))
+    highs = [v.astype(BF).astype(F32) for v in (by_weight, by_bias)]
+    split = jnp.concatenate(
+        [highs[0], by_weight - highs[0], highs[1], by_bias - highs[1]], axis=1
+    ).astype(BF)
+    tap = lax.broadcasted_iota(jnp.int32, (9, 256), 0)
+    at = lax.broadcasted_iota(jnp.int32, (9, 256), 1)
+    same = at // 16 == tap // 3
+    dx = tap % 3
+    place = at % 16
+    for j in range(8):
+        to = j + dx - 1
+        to = jnp.where(to == 8, 8, jnp.where(to == -1, 9, to))
+        pick = (same & (place == to)).astype(F32)
+        off = place == 12
+        if j == 7:
+            off = off | ((place == 10) & (dx == 2))
+        if j == 0:
+            off = off | ((place == 11) & (dx == 0))
+        drop = jnp.where(same & off, -1.0, 0.0)
+        picks = jnp.concatenate([pick, pick, drop, drop], axis=0).astype(BF)
+        value = bias + jnp.dot(split, picks, preferred_element_type=F32)
+        for h in range(2):
+            b_ref[h, pl.ds(j, C, stride=8), :] = value[:, h * 128 : (h + 1) * 128]
+    block = jnp.concatenate([b_ref[0], b_ref[1]], axis=1)
+    for r in range(STEP):
+        lift_ref[r] = (pltpu.roll(block, 16 * r, 1) if r else block).astype(BF)
+
+
+def mix_matrices(depth_kernel, mix_weight, mix_bias, lift_weight, lift_bias):
     return pl.pallas_call(
         mix_kernel,
-        out_shape=jax.ShapeDtypeStruct((LAYERS, 3, 192, 256), BF),
-        in_specs=[VMEM, VMEM, VMEM],
-        out_specs=VMEM,
+        out_shape=(
+            jax.ShapeDtypeStruct((LAYERS - 1, 3, 192, 256), BF),
+            jax.ShapeDtypeStruct((STEP, 192, 256), BF),
+        ),
+        in_specs=[VMEM] * 5,
+        out_specs=(VMEM, VMEM),
+        scratch_shapes=[pltpu.VMEM((2, 192, 128), F32)],
         cost_estimate=pl.CostEstimate(flops=20_000_000, bytes_accessed=1_000_000, transcendentals=0),
         name="mix_matrices",
-    )(depth_kernel, mix_weight, mix_bias)
+    )(depth_kernel.transpose(2, 0, 1), mix_weight, mix_bias, lift_weight.reshape(1, C), lift_bias.reshape(1, C))
 
 
 def denoise_kernel(*refs, NA, UN):
@@ -89,7 +137,7 @@
     return (cols == 8 * (at % 128) + 2 * n + at // 128).astype(F32).astype(BF)
 
 
-def to_groups(edge_ref, mv_ref, halo_ref, w_ref, lw_ref, lb_ref, ow_ref, out_ref, x_ref, f_ref, m_ref, *accs):
+def to_groups(edge_ref, mv_ref, halo_ref, w_ref, w0_ref, lw_ref, lb_ref, ow_ref, out_ref, after_ref, x_ref, f_ref, m_ref, t_ref, *accs):
     for n in range(4):
         for k in range(4):
             tile = group_tile(n, k, False)
@@ -113,7 +161,7 @@
                     ]
 
 
-def from_groups(edge_ref, mv_ref, halo_ref, w_ref, lw_ref, lb_ref, ow_ref, out_ref, x_ref, f_ref, m_ref, *accs):
+def from_groups(edge_ref, mv_ref, halo_ref, w_ref, w0_ref, lw_ref, lb_ref, ow_ref, out_ref, after_ref, x_ref, f_ref, m_ref, t_ref, *accs):
     def rows(p, n):
         parts = [
             [m_ref[p, h, pl.ds(8 * HALO + 2 * n + jj, R, stride=8), :] for jj in range(2)]
@@ -138,7 +186,7 @@
 
 
 def denoise_body(
-    edge_ref, mv_ref, halo_ref, w_ref, lw_ref, lb_ref, ow_ref, out_ref, x_ref, f_ref, m_ref, *accs, NA, UN
+    edge_ref, mv_ref, halo_ref, w_ref, w0_ref, lw_ref, lb_ref, ow_ref, out_ref, after_ref, x_ref, f_ref, m_ref, t_ref, *accs, NA, UN
 ):
     accs = (accs[:NA], accs[NA:])
     lanes = lax.broadcasted_iota(jnp.int32, (C, 128), 1)
@@ -164,36 +212,98 @@
         halo = jnp.concatenate([jnp.concatenate(right, 1), jnp.concatenate(left, 1)], 0)
         x_ref[p, y, 192:240, :] = halo.astype(BF)
 
-    def lift_row(y, _):
+    sub = lax.broadcasted_iota(jnp.int32, (8, 128), 0)
+    lane = lax.broadcasted_iota(jnp.int32, (8, 128), 1)
+    bias_rows = (sub == 5) | (sub == 6)
+    rest = bias_rows | ((sub == 2) & (lane == 127)) | ((sub == 3) & (lane == 0))
+    rest = rest.astype(F32)
+    for p in range(2):
+        for h in range(2):
+            m_ref[p, h, 8 * RH :, :] = jnp.zeros((8 * (RP - RH), 128), F32)
+
+    def frame_row(y, _):
         for p in range(2):
-            m = movie_row(p, y)
-            x_ref[p, y, 240:256, :] = ones
-            put(p, y, jnp.concatenate([m * lw_ref[c] + lb_ref[c] for c in range(C)], axis=0), p)
+            parts = []
+            for h in range(2):
+                m = m_ref[p, h, pl.ds(pl.multiple_of(y * 8, 8), 8), :]
+                right = jnp.where((sub == 0) & (lane < 127), pltpu.roll(m, 127, 1), 0.0)
+                left = pltpu.roll(pltpu.roll(m, 1, 1), 2, 0)
+                left = jnp.where((sub == 1) & (lane > 0), left, 0.0)
+                parts.append(jnp.concatenate([m, right + left + rest], axis=0))
+            at = pl.multiple_of(y * 16, 16)
+            t_ref[p, pl.ds(at, 16), :] = jnp.concatenate(parts, axis=1).astype(BF)
         return 0
 
-    lax.fori_loop(0, RH, lift_row, 0)
-
-    def zero_edges():
+    lax.fori_loop(0, RP, frame_row, 0, unroll=4)
+    off_row = (lax.broadcasted_iota(jnp.int32, (16, 256), 0) == 12).astype(F32).astype(BF)
+
+    def at_edges(store):
         for side, rows in ((0, range(HALO)), (1, range(RH - HALO, RH))):
 
             @pl.when(edge_ref[side] == 1)
             def _():
                 for p in range(2):
                     for y in rows:
-                        x_ref[p, y, 0:240, :] = jnp.zeros((240, 256), BF)
-
-    zero_edges()
-
-    for layer in range(LAYERS):
+                        store(p, y)
+
+    def off_frame(p, y):
+        t_ref[p, 16 * y : 16 * y + 16, :] = off_row
+
+    def off_features(p, y):
+        x_ref[p, y, 0:240, :] = jnp.zeros((240, 256), BF)
+
+    at_edges(off_frame)
+
+    def first_layer(b, _):
+        y0 = b * STEP
+        for p in range(2):
+            rows = t_ref[p, pl.ds(pl.multiple_of(y0 * 16, 16), 256), :]
+            pltpu.matmul_push_rhs(rows, 0, p)
+
+        def issue(r):
+            for p in range(2):
+                pltpu.matmul_acc_lhs(
+                    accs[p][r % NA], w0_ref[r], load_staged_rhs=0 if r == 0 else None
+                )
+
+        def done(r):
+            y = y0 + r + 1
+            for p in range(2):
+                mixed = pltpu.matmul_pop(accs[p][r % NA])
+                m = movie_row(p, y)
+                new = [
+                    m * lw_ref[c] + lb_ref[c] + jnp.maximum(mixed[8 * c : 8 * c + 8], 0.0)
+                    for c in range(C)
+                ]
+                x_ref[p, y, 240:256, :] = ones
+                put(p, y, jnp.concatenate(new, axis=0), (r % 2) * 2 + p)
+
+        issue(0)
+        for r in range(1, STEP):
+            issue(r)
+            done(r - 1)
+        done(STEP - 1)
+        return 0
+
+    for p in range(2):
+        x_ref[p, 0, 240:256, :] = ones
+    lax.fori_loop(0, (RH + STEP - 3) // STEP, first_layer, 0)
+    at_edges(off_features)
+
+    for layer in range(1, LAYERS):
         lo, hi = layer + 1, RH - layer - 1
 
-        def tile(y, terms):
-            for p in range(2):
-                pltpu.matmul_push_rhs(x_ref[p, y], 0, p)
+        def push(y, a):
+            for p in range(2):
+                pltpu.matmul_push_rhs(x_ref[p, y], a % 2, p)
+
+        def tile(i, terms):
             for n, (dy, a) in enumerate(terms):
                 for p in range(2):
                     pltpu.matmul_acc_lhs(
-                        accs[p][a % NA], w_ref[layer, dy], load_staged_rhs=0 if n == 0 else None
+                        accs[p][a % NA],
+                        w_ref[layer - 1, dy],
+                        load_staged_rhs=i % 2 if n == 0 else None,
                     )
 
         def finish(y, a, slot):
@@ -213,11 +323,15 @@
                         m_ref[p, h, pl.ds(at, 8), :] = total[:, h * 128 : (h + 1) * 128]
 
         def step(y, i):
-            tile(y, [(2, i - 1), (1, i), (0, i + 1)])
+            push(y + 1, i + 1)
+            tile(i, [(2, i - 1), (1, i), (0, i + 1)])
             finish(y - 1, i - 1, i % 2)
 
-        tile(lo - 1, [(0, 0)])
-        tile(lo, [(0, 1), (1, 0)])
+        push(lo - 1, 1)
+        push(lo, 0)
+        tile(1, [(0, 0)])
+        push(lo + 1, 1)
+        tile(0, [(0, 1), (1, 0)])
         n_main = hi - lo - 2
 
         def body(b, _):
@@ -230,84 +344,113 @@
         for u in range(n_main - n_loop * UN):
             step(lo + 1 + n_loop * UN + u, 1 + u)
         i = n_main + 1
-        tile(hi - 1, [(2, i - 1), (1, i)])
+        push(hi, i + 1)
+        tile(i, [(2, i - 1), (1, i)])
         finish(hi - 2, i - 1, 0)
-        tile(hi, [(2, i)])
+        tile(i + 1, [(2, i)])
         finish(hi - 1, i, 1)
         if layer < LAYERS - 1:
-            zero_edges()
-
-
-def denoise(edge, movie, halo, mats, lift_weight, lift_bias, out_weight, NA=4, UN=8):
+            at_edges(off_features)
+
+    after_ref[...] = jnp.zeros(after_ref.shape, F32)
+
+
+def denoise(edge, movie, halo, mats, lift_mats, lift_weight, lift_bias, out_weight, NA=4, UN=8):
     return pl.pallas_call(
         functools.partial(denoise_kernel, NA=NA, UN=UN),
-        out_shape=jax.ShapeDtypeStruct((8, 4, R, 128), BF),
-        in_specs=[SMEM, VMEM, VMEM, VMEM, SMEM, SMEM, SMEM],
-        out_specs=VMEM,
+        out_shape=(
+            jax.ShapeDtypeStruct((8, 4, R, 128), BF),
+            jax.ShapeDtypeStruct((8, 128), F32),
+        ),
+        in_specs=[SMEM, VMEM, VMEM, VMEM, VMEM, SMEM, SMEM, SMEM],
+        out_specs=(VMEM, VMEM),
         scratch_shapes=[
-            pltpu.VMEM((2, RH, 256, 256), BF),
+            pltpu.VMEM((2, RP, 256, 256), BF),
             pltpu.VMEM((4, 2, 192, 128), F32),
-            pltpu.VMEM((2, 2, RH * 8, 128), F32),
+            pltpu.VMEM((2, 2, RP * 8, 128), F32),
+            pltpu.VMEM((2, RP * 16, 256), BF),
         ],
         compiler_params=pltpu.CompilerParams(vmem_limit_bytes=56 * 2**20),
         name="denoise",
-    )(edge, movie, halo, mats, lift_weight, lift_bias, out_weight)
-
-
-def relay_kernel(foot_ref, own_row_ref, own_col_ref, id_ref, after_ref, out_ref, hot_ref, ids_ref, s_ref):
-    slots = foot_ref.shape[0]
-    own_row = own_row_ref[...]
-    own_col = own_col_ref[...]
-    before = lax.broadcasted_iota(jnp.int32, (slots, slots), 0) < lax.broadcasted_iota(
-        jnp.int32, (slots, slots), 1
-    )
-    rank = jnp.sum(((own_row == own_col) & before).astype(jnp.int32), axis=0, keepdims=True)
-    place = own_row * CAP + rank
-    hot = place == lax.broadcasted_iota(jnp.int32, hot_ref.shape, 0)
-    hot_ref[...] = hot.astype(F32).astype(BF)
-    ids = id_ref[...]
-    second = lax.broadcasted_iota(jnp.int32, (slots, 2), 1) == 1
-    ids_ref[...] = jnp.where(second, ids % ID_BASE, ids // ID_BASE).astype(F32).astype(BF)
-
-    def part(g, _):
-        r0 = pl.multiple_of(g * 16, 16)
+    )(edge, movie, halo, mats, lift_mats, lift_weight, lift_bias, out_weight)
+
+
+def relay_kernel(foot_any, after_ref, out_any, in_ref, s_ref, o_ref, in_sem, out_sem):
+    slots = foot_any.shape[0]
+    parts = R // 16
+    pitch = slots + 8
+
+    def load(g):
+        return pltpu.make_async_copy(
+            foot_any.at[:, pl.ds(16 * g, 16), :], in_ref.at[g % 2], in_sem.at[g % 2]
+        )
+
+    def save(g):
+        return pltpu.make_async_copy(
+            o_ref.at[g % 2], out_any.at[pl.ds(8 * g, 8)], out_sem.at[g % 2]
+        )
+
+    load(0).start()
+
+    for g in range(parts):
+        if g + 1 < parts:
+            load(g + 1).start()
+        load(g).wait()
 
         def slot(b, _):
             for u in range(16):
                 s = b * 16 + u
-                s_ref[pl.ds(s, 16, stride=slots), :] = foot_ref[s, pl.ds(r0, 16), :].astype(F32)
+                s_ref[pl.ds(s, 16, stride=pitch), :] = in_ref[g % 2, s].astype(F32)
             return 0
 
         lax.fori_loop(0, slots // 16, slot, 0)
+        if g >= 2:
+            save(g - 2).wait()
         for q in range(8):
-            two = [s_ref[(2 * q + e) * slots : (2 * q + e + 1) * slots, :] for e in range(2)]
-            out_ref[g * 8 + q] = jnp.concatenate(two, axis=1).astype(BF)
-        return 0
-
-    lax.fori_loop(0, R // 16, part, 0)
-
-
-def relay(footprints, slot_owner, slot_neuron, n_dev, after):
+            two = [s_ref[(2 * q + e) * pitch : (2 * q + e) * pitch + slots, :] for e in range(2)]
+            o_ref[g % 2, q] = jnp.concatenate(two, axis=1).astype(BF)
+        save(g).start()
+    for g in range(parts - 2, parts):
+        save(g).wait()
+
+
+def relay(footprints, after):
     slots = footprints.shape[0]
     return pl.pallas_call(
         relay_kernel,
-        out_shape=(
-            jax.ShapeDtypeStruct((R // 2, slots, 256), BF),
-            jax.ShapeDtypeStruct((n_dev * CAP, slots), BF),
-            jax.ShapeDtypeStruct((slots, 2), BF),
-        ),
-        in_specs=[VMEM] * 4 + [pl.BlockSpec(memory_space=pl.ANY)],
-        out_specs=(VMEM, VMEM, VMEM),
-        scratch_shapes=[pltpu.VMEM((16 * slots, 128), F32)],
-        compiler_params=pltpu.CompilerParams(vmem_limit_bytes=24 * 2**20),
+        out_shape=jax.ShapeDtypeStruct((R // 2, slots, 256), BF),
+        in_specs=[HBM, VMEM],
+        out_specs=HBM,
+        scratch_shapes=[
+            pltpu.VMEM((2, slots, 16, 128), BF),
+            pltpu.VMEM((16 * (slots + 8), 128), F32),
+            pltpu.VMEM((2, 8, slots, 256), BF),
+            pltpu.SemaphoreType.DMA((2,)),
+            pltpu.SemaphoreType.DMA((2,)),
+        ],
+        compiler_params=pltpu.CompilerParams(vmem_limit_bytes=61 * 2**20),
         cost_estimate=pl.CostEstimate(flops=20_000_000, bytes_accessed=12_000_000, transcendentals=0),
         name="relay",
-    )(footprints, slot_owner.reshape(1, slots), slot_owner, slot_neuron.reshape(slots, 1), after)
-
-
-def trace_kernel(got_ref, tk_ref, foot_ref, hot_ref, ids_ref, filt_ref, send_ref, g_ref):
+    )(footprints, after)
+
+
+def trace_kernel(
+    got_ref, tk_ref, foot_any, own_ref, id_ref, filt_ref, send_ref, g_ref, foot_ref, sem
+):
     half = 4
-    for r0 in range(0, R, 16):
+    pitch = NT + 8
+    parts = R // 16
+    copies = [
+        pltpu.make_async_copy(
+            foot_any.at[pl.ds(8 * g, 8)], foot_ref.at[pl.ds(8 * g, 8)], sem.at[g]
+        )
+        for g in range(parts)
+    ]
+    for copy in copies:
+        copy.start()
+    traces = jnp.zeros((foot_ref.shape[1], NT), F32)
+    for g in range(parts):
+        r0 = 16 * g
         frames = [got_ref[t, r0 : r0 + 16, :].astype(F32) for t in range(NT)]
         for t in range(NT):
             total = None
@@ -318,33 +461,56 @@
                     total = term if total is None else total + term
             out = total.astype(BF)
             filt_ref[t, r0 : r0 + 16, :] = out
-            g_ref[pl.ds(r0 * NT + t, 16, stride=NT), :] = out.astype(F32)
-    total = jnp.zeros((foot_ref.shape[1], NT), F32)
-    for q in range(R // 2):
-        two = [g_ref[(2 * q + e) * NT : (2 * q + e + 1) * NT, :] for e in range(2)]
-        rows = jnp.concatenate(two, axis=1).astype(BF)
-        total = total + lax.dot_general(
-            foot_ref[q], rows, (((1,), (1,)), ((), ())), preferred_element_type=F32
-        )
-    sending = jnp.concatenate([total.astype(BF).astype(F32), ids_ref[...].astype(F32)], axis=1)
+            g_ref[pl.ds(t, 16, stride=pitch), :] = out.astype(F32)
+        copies[g].wait()
+        for q in range(8):
+            two = [g_ref[(2 * q + e) * pitch : (2 * q + e) * pitch + NT, :] for e in range(2)]
+            rows = jnp.concatenate(two, axis=1).astype(BF)
+            traces = traces + lax.dot_general(
+                foot_ref[8 * g + q], rows, (((1,), (1,)), ((), ())), preferred_element_type=F32
+            )
+    slots = foot_any.shape[1]
+    own_row = own_ref[...]
+    r_of = lax.broadcasted_iota(jnp.int32, (slots, slots), 0)
+    c_of = lax.broadcasted_iota(jnp.int32, (slots, slots), 1)
+
+    def column(row):
+        picked = jnp.where(r_of == c_of, row.astype(F32), 0.0)
+        return jnp.sum(picked, axis=1, keepdims=True).astype(jnp.int32)
+
+    own_col = column(own_row)
+    rank = jnp.where((own_row == own_col) & (r_of < c_of), 1.0, 0.0)
+    rank = jnp.sum(rank, axis=0, keepdims=True).astype(jnp.int32)
+    place = own_row * CAP + rank
+    hot = place == lax.broadcasted_iota(jnp.int32, (send_ref.shape[0], slots), 0)
+    hot = hot.astype(F32).astype(BF)
+    ids = column(id_ref[...])
+    second = lax.broadcasted_iota(jnp.int32, (slots, 2), 1) == 1
+    ids = jnp.where(second, ids % ID_BASE, ids // ID_BASE).astype(F32)
+    sending = jnp.concatenate([traces, ids], axis=1)
     send_ref[...] = jnp.dot(
-        hot_ref[...], sending.astype(BF), preferred_element_type=F32
+        hot, sending.astype(BF), preferred_element_type=F32
     ).astype(BF)
 
 
-def trace(received, temporal_kernel, foot, hot, ids):
+def trace(received, temporal_kernel, foot, slot_owner, slot_neuron, n_dev):
+    slots = foot.shape[1]
     return pl.pallas_call(
         trace_kernel,
         out_shape=(
             jax.ShapeDtypeStruct((NT, R, 128), BF),
-            jax.ShapeDtypeStruct((hot.shape[0], NT + 2), BF),
+            jax.ShapeDtypeStruct((n_dev * CAP, NT + 2), BF),
         ),
-        in_specs=[VMEM, SMEM, VMEM, VMEM, VMEM],
+        in_specs=[VMEM, SMEM, HBM, VMEM, VMEM],
         out_specs=(VMEM, VMEM),
-        scratch_shapes=[pltpu.VMEM((R * NT, 128), F32)],
-        compiler_params=pltpu.CompilerParams(vmem_limit_bytes=24 * 2**20),
+        scratch_shapes=[
+            pltpu.VMEM((16 * (NT + 8), 128), F32),
+            pltpu.VMEM(foot.shape, BF),
+            pltpu.SemaphoreType.DMA((R // 16,)),
+        ],
+        compiler_params=pltpu.CompilerParams(vmem_limit_bytes=50 * 2**20),
         name="trace",
-    )(received, temporal_kernel, foot, hot, ids)
+    )(received, temporal_kernel, foot, slot_owner.reshape(1, slots), slot_neuron.reshape(1, slots))
 
 
 def gather_kernel(got_ref, out_ref):
@@ -389,14 +555,16 @@
     halo = jnp.concatenate([low, high], axis=1).reshape(2, 4 * HALO, W)
     halo = jnp.pad(halo, ((0, 0), (0, 16 - 4 * HALO), (0, 0)))
     edge = jnp.stack([me == 0, me == n_tile - 1]).astype(jnp.int32)
-    mats = mix_matrices(depth_kernel, mix_weight, mix_bias)
-    denoised = denoise(
-        edge, movie.reshape(2, 2 * R, W), halo, mats, lift_weight, lift_bias, out_weight
+    mats, lift_mats = mix_matrices(depth_kernel, mix_weight, mix_bias, lift_weight, lift_bias)
+    denoised, after = denoise(
+        edge, movie.reshape(2, 2 * R, W), halo, mats, lift_mats, lift_weight, lift_bias, out_weight
     )
     n_dev = lax.axis_size("tm") * n_tile
     received = lax.all_to_all(denoised, "tm", 0, 0, tiled=True)
-    foot, hot, ids = relay(footprints, slot_owner, slot_neuron, n_dev, denoised)
-    filtered, outgoing = trace(received.reshape(NT, R, 128), temporal_kernel, foot, hot, ids)
+    foot = relay(footprints, after)
+    filtered, outgoing = trace(
+        received.reshape(NT, R, 128), temporal_kernel, foot, slot_owner, slot_neuron, n_dev
+    )
     arriving = lax.all_to_all(
         outgoing.reshape(n_dev, CAP, NT + 2), ("tm", "tile"), 0, 0, tiled=True
     )

time: 110 us -> 89.9 us (0.82)
  Pallas kernels: 65 us -> 52 us
  local copies, waits for them, and re-layouts: 10.6 us -> 1.58 us
  waiting for transfers between devices: 0.01 us -> 3.24 us
  blocking collectives: 20.8 us -> 19.2 us
    pallas_call x1, Pallas kernels: 50.3 us -> 36.6 us  [denoise(): pl.pallas_call(functools.partial(denoise_kernel, NA=NA, UN=UN), out_shape...]
    unnamed x16 -> x6, local copies, waits for them, and re-layouts: 8.93 us -> 0.01 us
    all_to_all x1, waiting for transfers between devices: 0.01 us -> 3.17 us  [local(): received = lax.all_to_all(denoised, 'tm', 0, 0, tiled=True)]
    pallas_call x1, Pallas kernels: 2.75 us -> 4.5 us  [trace(): pl.pallas_call(trace_kernel, out_shape=(jax.ShapeDtypeStruct((NT, R, 128)...]
    all_to_all x1, blocking collectives: 20.8 us -> 19.2 us  [local(): lax.all_to_all(outgoing.reshape(n_dev, CAP, NT + 2), ('tm', 'tile'), 0, 0...]
  transfers between devices with their start and end apart: 3 -> 3, of which waited for: 0 -> 2; matrix products, arithmetic and copies ran while one was open for 2% -> 1% of each run, Pallas kernels for 9% -> 10%
where the time goes in v3:
time: 89.9 us; the launch traced here: 89.4 us
  Pallas kernels  52 us (58%)
  blocking collectives  19.2 us (21%)
  starting transfers between devices  12 us (13%)
  waiting for transfers between devices  3.24 us (4%)
  local copies, waits for them, and re-layouts  1.58 us (2%)
    pallas_call x1, Pallas kernels, denoise(): pl.pallas_call(functools.partial(denoise_kernel, NA=NA, UN=UN), out_shape...  36.6 us
    all_to_all x1, blocking collectives, local(): lax.all_to_all(outgoing.reshape(n_dev, CAP, NT + 2), ('tm', 'tile'), 0, 0...  19.2 us
    all_to_all x1, starting transfers between devices, local(): received = lax.all_to_all(denoised, 'tm', 0, 0, tiled=True)  6.38 us
    pallas_call x1, Pallas kernels, relay(): pl.pallas_call(relay_kernel, out_shape=jax.ShapeDtypeStruct((R // 2, slot...  6.16 us
    pallas_call x1, Pallas kernels, trace(): pl.pallas_call(trace_kernel, out_shape=(jax.ShapeDtypeStruct((NT, R, 128)...  4.5 us
    ppermute x1, starting transfers between devices, local(): low = lax.ppermute(movie[:, R - HALO:], 'tile', up)  4.36 us
    all_to_all x1, waiting for transfers between devices, local(): received = lax.all_to_all(denoised, 'tm', 0, 0, tiled=True)  3.17 us
    pallas_call x1, Pallas kernels, mix_matrices(): pl.pallas_call(mix_kernel, out_shape=(jax.ShapeDtypeStruct((LAYERS - 1, 3...  2.82 us
  transfers between devices with their start and end apart: 3, of which 2 were waited for; matrix products, arithmetic and copies ran while one was open for 1% of the time, Pallas kernels for 10%

profile of v3, /device:TPU:1, one launch (start us, length us, event | category | flops | bytes accessed | tf_op | source)
XLA Modules:
  0.0 89.4 jit_solution(10840251860241860684)
XLA Ops:
  0.6 0.9 %fusion = (bf16[4,3,1024]{2,1,0:T(4,128)(2,1)S(1)}, bf16[4,3,1024]{2,1,0:T(4,128)(2,1)S(1)}) fusion(bf16[4,64,1024]{2,1,0:T(8,128)(2,1)} %param.11), kind=kLoop, calls=%fused_computation.2 | loop fusion | bytes 98304 | tf_op jit(solution)/shard_map/slice | solution.py:553
  1.5 4.4 %collective-permute-start = (bf16[4,3,1024]{2,1,0:T(4,128)(2,1)S(1)}, bf16[4,3,1024]{2,1,0:T(4,128)(2,1)S(1)}, u32[]{:S(2)}, u32[]{:S(2)}) collective-permute-start(bf16[4,3,1024]{2,1,0:T(4,128)(2,1)S(1)} %get-tuple-element.14), channel_id=1, source_target_pairs={{0,1},{1,2},{2,3},{3,4},{4,5},{5,6},{6,7},{7,8},{8,9},{9,10},{10,1... | collective-permute-start | bytes 73736 | tf_op jit(solution)/shard_map/ppermute | solution.py:553
  5.9 1.3 %collective-permute-start.1 = (bf16[4,3,1024]{2,1,0:T(4,128)(2,1)S(1)}, bf16[4,3,1024]{2,1,0:T(4,128)(2,1)S(1)}, u32[]{:S(2)}, u32[]{:S(2)}) collective-permute-start(bf16[4,3,1024]{2,1,0:T(4,128)(2,1)S(1)} %get-tuple-element.15), channel_id=1, source_target_pairs={{1,0},{2,1},{3,2},{4,3},{5,4},{6,5},{7,6},{8,7},{9,8},{10,9},{11,1... | collective-permute-start | bytes 73736 | tf_op jit(solution)/shard_map/ppermute | solution.py:554
  7.2 0.7 add_convert_fusion.refs_0_
  7.9 2.8 %mix_matrices.1 = (bf16[2,3,192,256]{3,2,1,0:T(8,128)(2,1)}, bf16[14,192,256]{2,1,0:T(8,128)(2,1)}) custom-call(f32[9,3,24]{2,1,0:T(4,128)} %bitcast.21, bf16[3,24,24]{2,1,0:T(8,128)(2,1)} %mix_ref.1, f32[3,24]{1,0:T(4,128)} %bias_ref.1, f32[1,24]{1,0:T(1,128)} %bitcast.19, f32[1,24]{1,0:T(1,128)} %bitcast.20), custom_call_target="tpu_custom_call" | custom-call | flops 20000000 | bytes 1000000 | tf_op jit(solution)/shard_map/mix_matrices/pallas_call | solution.py:108
  10.7 0.0 collective-permute-done
  10.7 0.1 collective-permute-done.1
  10.8 0.6 pad.4.refs_2_
  11.5 36.6 %denoise.1 = (bf16[8,4,64,128]{3,2,1,0:T(8,128)(2,1)}, f32[8,128]{1,0:T(8,128)}) custom-call(s32[2]{0:T(128)} %add_convert_fusion.refs_0_, bf16[2,128,1024]{2,1,0:T(8,128)(2,1)} %bitcast.16, bf16[2,16,1024]{2,1,0:T(8,128)(2,1)} %pad.4.refs_2_, bf16[2,3,192,256]{3,2,1,0:T(8,128)(2,1)} %get-tuple-element.8.refs_3_, ...), custom_call_target="tpu_custom_call" | custom-call | tf_op jit(solution)/shard_map/denoise/pallas_call | solution.py:359
  48.0 6.4 %all-to-all-start = ((bf16[8,4,64,128]{3,2,1,0:T(8,128)(2,1)}), bf16[8,4,64,128]{3,2,1,0:T(8,128)(2,1)S(1)}, u32[]{:S(2)}, u32[]{:S(2)}) async-start(bf16[8,4,64,128]{3,2,1,0:T(8,128)(2,1)} %get-tuple-element.10), calls=%async_computation | async-start | bytes 1048576 | tf_op jit(solution)/shard_map/all_to_all | solution.py:563
  54.4 0.0 copy-start
  54.4 0.0 copy-start.1
  54.4 0.0 copy-start.2
  54.4 6.2 %relay.1.foot_any = bf16[32,256,256]{2,1,0:T(8,128)(2,1)} custom-call(bf16[256,64,128]{2,1,0:T(8,128)(2,1)} %foot_any.1, f32[8,128]{1,0:T(8,128)} %get-tuple-element.11.after_ref), custom_call_target="tpu_custom_call" | custom-call | flops 20000000 | bytes 12000000 | tf_op jit(solution)/shard_map/relay/pallas_call | solution.py:419
  60.6 3.2 %all-to-all-done = bf16[8,4,64,128]{3,2,1,0:T(8,128)(2,1)S(1)} async-done(((bf16[8,4,64,128]{3,2,1,0:T(8,128)(2,1)}), bf16[8,4,64,128]{3,2,1,0:T(8,128)(2,1)S(1)}, u32[]{:S(2)}, u32[]{:S(2)}) %all-to-all-start) | async-done | bytes 524320 | tf_op jit(solution)/shard_map/all_to_all | solution.py:563
  63.8 0.0 copy-done
  63.8 0.0 copy-done.1
  63.8 0.0 copy-done.2
  63.8 4.5 %trace.1 = (bf16[32,64,128]{2,1,0:T(8,128)(2,1)}, bf16[512,34]{1,0:T(8,128)(2,1)S(1)}) custom-call(bf16[32,64,128]{2,1,0:T(8,128)(2,1)S(1)} %bitcast.12, f32[9]{0:T(128)S(1)} %copy-done.2, bf16[32,256,256]{2,1,0:T(8,128)(2,1)} %relay.1.foot_any, s32[1,256]{1,0:T(1,128)S(1)} %bitcast.14, s32[1,256]{1,0:T(1,128)S(1)} %bitcast.15), custom_call_target="tpu_custom_call" | custom-call | tf_op jit(solution)/shard_map/trace/pallas_call | solution.py:498
  68.3 19.2 %all_to_all.10 = bf16[128,4,34]{2,1,0:T(4,128)(2,1)} all-to-all(bf16[128,4,34]{2,1,0:T(4,128)(2,1)S(1)} %bitcast.13), channel_id=1, replica_groups=mesh['tm'=8,'tile'=16] {'tm','tile'}, dimensions={0} | all-to-all | bytes 69632 | tf_op jit(solution)/shard_map/all_to_all | solution.py:568
  87.5 1.9 %gather.1 = f32[32,320]{1,0:T(8,128)} custom-call(bf16[512,34]{1,0:T(8,128)(2,1)} %bitcast.17), custom_call_target="tpu_custom_call" | custom-call | tf_op jit(solution)/shard_map/gather/pallas_call | solution.py:527
  (2 shorter events, 0.1 us)
Async XLA Ops:
  1.5 9.2 %collective-permute-start = (bf16[4,3,1024]{2,1,0:T(4,128)(2,1)S(1)}, bf16[4,3,1024]{2,1,0:T(4,128)(2,1)S(1)}, u32[]{:S(2)}, u32[]{:S(2)}) collective-permute-start(bf16[4,3,1024]{2,1,0:T(4,128)(2,1)S(1)} %get-tuple-element.14), channel_id=1, source_target_pairs={{0,1},{1,2},{2,3},{3,4},{4,5},{5,6},{6,7},{7,8},{8,9},{9,10},{10,1... | collective-permute-start | bytes 73736 | tf_op jit(solution)/shard_map/ppermute | solution.py:553
  5.9 4.8 %collective-permute-start.1 = (bf16[4,3,1024]{2,1,0:T(4,128)(2,1)S(1)}, bf16[4,3,1024]{2,1,0:T(4,128)(2,1)S(1)}, u32[]{:S(2)}, u32[]{:S(2)}) collective-permute-start(bf16[4,3,1024]{2,1,0:T(4,128)(2,1)S(1)} %get-tuple-element.15), channel_id=1, source_target_pairs={{1,0},{2,1},{3,2},{4,3},{5,4},{6,5},{7,6},{8,7},{9,8},{10,9},{11,1... | collective-permute-start | bytes 73736 | tf_op jit(solution)/shard_map/ppermute | solution.py:554
  48.0 15.7 %all-to-all-start = ((bf16[8,4,64,128]{3,2,1,0:T(8,128)(2,1)}), bf16[8,4,64,128]{3,2,1,0:T(8,128)(2,1)S(1)}, u32[]{:S(2)}, u32[]{:S(2)}) async-start(bf16[8,4,64,128]{3,2,1,0:T(8,128)(2,1)} %get-tuple-element.10), calls=%async_computation | async-start | bytes 1048576 | tf_op jit(solution)/shard_map/all_to_all | solution.py:563
  54.4 9.4 %copy-start = (s32[256,1]{0,1:T(1,128)S(1)}, s32[256,1]{0,1:T(1,128)}, u32[]{:S(2)}) copy-start(s32[256,1]{0,1:T(1,128)} %param.20) | copy-start | bytes 3076
  54.4 9.4 %copy-start.1 = (s32[256]{0:T(256)S(1)}, s32[256]{0:T(256)}, u32[]{:S(2)}) copy-start(s32[256]{0:T(256)} %param.21) | copy-start | bytes 3076
  54.4 9.4 %copy-start.2 = (f32[9]{0:T(128)S(1)}, f32[9]{0:T(128)}, u32[]{:S(2)}) copy-start(f32[9]{0:T(128)} %tk_ref.1) | copy-start | bytes 112

commit v4 on v3

--- a/solution.py
+++ b/solution.py
@@ -333,16 +333,17 @@
         push(lo + 1, 1)
         tile(0, [(0, 1), (1, 0)])
         n_main = hi - lo - 2
+        un = UN[layer - 1]
 
         def body(b, _):
-            for u in range(UN):
-                step(lo + 1 + b * UN + u, 1 + u)
+            for u in range(un):
+                step(lo + 1 + b * un + u, 1 + u)
             return 0
 
-        n_loop = n_main // UN
+        n_loop = n_main // un
         lax.fori_loop(0, n_loop, body, 0)
-        for u in range(n_main - n_loop * UN):
-            step(lo + 1 + n_loop * UN + u, 1 + u)
+        for u in range(n_main - n_loop * un):
+            step(lo + 1 + n_loop * un + u, 1 + u)
         i = n_main + 1
         push(hi, i + 1)
         tile(i, [(2, i - 1), (1, i)])
@@ -355,7 +356,7 @@
     after_ref[...] = jnp.zeros(after_ref.shape, F32)
 
 
-def denoise(edge, movie, halo, mats, lift_mats, lift_weight, lift_bias, out_weight, NA=4, UN=8):
+def denoise(edge, movie, halo, mats, lift_mats, lift_weight, lift_bias, out_weight, NA=4, UN=(16, 20)):
     return pl.pallas_call(
         functools.partial(denoise_kernel, NA=NA, UN=UN),
         out_shape=(

time: 89.9 us -> 89.2 us (level)
  no operation moved by 1% of the time
where the time goes in v4:
time: 89.2 us; the launch traced here: 88.7 us
  Pallas kernels  51.2 us (57%)
  blocking collectives  19.2 us (22%)
  starting transfers between devices  12.1 us (14%)
  waiting for transfers between devices  3.24 us (4%)
  local copies, waits for them, and re-layouts  1.58 us (2%)
    pallas_call x1, Pallas kernels, denoise(): pl.pallas_call(functools.partial(denoise_kernel, NA=NA, UN=UN), out_shape...  35.8 us
    all_to_all x1, blocking collectives, local(): lax.all_to_all(outgoing.reshape(n_dev, CAP, NT + 2), ('tm', 'tile'), 0, 0...  19.2 us
    all_to_all x1, starting transfers between devices, local(): received = lax.all_to_all(denoised, 'tm', 0, 0, tiled=True)  6.4 us
    pallas_call x1, Pallas kernels, relay(): pl.pallas_call(relay_kernel, out_shape=jax.ShapeDtypeStruct((R // 2, slot...  6.16 us
    pallas_call x1, Pallas kernels, trace(): pl.pallas_call(trace_kernel, out_shape=(jax.ShapeDtypeStruct((NT, R, 128)...  4.5 us
    ppermute x1, starting transfers between devices, local(): low = lax.ppermute(movie[:, R - HALO:], 'tile', up)  4.36 us
    all_to_all x1, waiting for transfers between devices, local(): received = lax.all_to_all(denoised, 'tm', 0, 0, tiled=True)  3.17 us
    pallas_call x1, Pallas kernels, mix_matrices(): pl.pallas_call(mix_kernel, out_shape=(jax.ShapeDtypeStruct((LAYERS - 1, 3...  2.82 us
  transfers between devices with their start and end apart: 3, of which 2 were waited for; matrix products, arithmetic and copies ran while one was open for 1% of the time, Pallas kernels for 10%

profile of v4, /device:TPU:1, one launch (start us, length us, event | category | flops | bytes accessed | tf_op | source)
XLA Modules:
  0.0 88.7 jit_solution(13582015397540569920)
XLA Ops:
  0.6 0.9 %fusion = (bf16[4,3,1024]{2,1,0:T(4,128)(2,1)S(1)}, bf16[4,3,1024]{2,1,0:T(4,128)(2,1)S(1)}) fusion(bf16[4,64,1024]{2,1,0:T(8,128)(2,1)} %param.11), kind=kLoop, calls=%fused_computation.2 | loop fusion | bytes 98304 | tf_op jit(solution)/shard_map/slice | solution.py:554
  1.5 4.4 %collective-permute-start = (bf16[4,3,1024]{2,1,0:T(4,128)(2,1)S(1)}, bf16[4,3,1024]{2,1,0:T(4,128)(2,1)S(1)}, u32[]{:S(2)}, u32[]{:S(2)}) collective-permute-start(bf16[4,3,1024]{2,1,0:T(4,128)(2,1)S(1)} %get-tuple-element.14), channel_id=1, source_target_pairs={{0,1},{1,2},{2,3},{3,4},{4,5},{5,6},{6,7},{7,8},{8,9},{9,10},{10,1... | collective-permute-start | bytes 73736 | tf_op jit(solution)/shard_map/ppermute | solution.py:554
  5.9 1.3 %collective-permute-start.1 = (bf16[4,3,1024]{2,1,0:T(4,128)(2,1)S(1)}, bf16[4,3,1024]{2,1,0:T(4,128)(2,1)S(1)}, u32[]{:S(2)}, u32[]{:S(2)}) collective-permute-start(bf16[4,3,1024]{2,1,0:T(4,128)(2,1)S(1)} %get-tuple-element.15), channel_id=1, source_target_pairs={{1,0},{2,1},{3,2},{4,3},{5,4},{6,5},{7,6},{8,7},{9,8},{10,9},{11,1... | collective-permute-start | bytes 73736 | tf_op jit(solution)/shard_map/ppermute | solution.py:555
  7.2 0.7 add_convert_fusion.refs_0_
  7.9 2.8 %mix_matrices.1 = (bf16[2,3,192,256]{3,2,1,0:T(8,128)(2,1)}, bf16[14,192,256]{2,1,0:T(8,128)(2,1)}) custom-call(f32[9,3,24]{2,1,0:T(4,128)} %bitcast.21, bf16[3,24,24]{2,1,0:T(8,128)(2,1)} %mix_ref.1, f32[3,24]{1,0:T(4,128)} %bias_ref.1, f32[1,24]{1,0:T(1,128)} %bitcast.19, f32[1,24]{1,0:T(1,128)} %bitcast.20), custom_call_target="tpu_custom_call" | custom-call | flops 20000000 | bytes 1000000 | tf_op jit(solution)/shard_map/mix_matrices/pallas_call | solution.py:108
  10.7 0.0 collective-permute-done
  10.7 0.1 collective-permute-done.1
  10.8 0.6 pad.4.refs_2_
  11.5 35.8 %denoise.1 = (bf16[8,4,64,128]{3,2,1,0:T(8,128)(2,1)}, f32[8,128]{1,0:T(8,128)}) custom-call(s32[2]{0:T(128)} %add_convert_fusion.refs_0_, bf16[2,128,1024]{2,1,0:T(8,128)(2,1)} %bitcast.16, bf16[2,16,1024]{2,1,0:T(8,128)(2,1)} %pad.4.refs_2_, bf16[2,3,192,256]{3,2,1,0:T(8,128)(2,1)} %get-tuple-element.8.refs_3_, ...), custom_call_target="tpu_custom_call" | custom-call | tf_op jit(solution)/shard_map/denoise/pallas_call | solution.py:360
  47.3 6.4 %all-to-all-start = ((bf16[8,4,64,128]{3,2,1,0:T(8,128)(2,1)}), bf16[8,4,64,128]{3,2,1,0:T(8,128)(2,1)S(1)}, u32[]{:S(2)}, u32[]{:S(2)}) async-start(bf16[8,4,64,128]{3,2,1,0:T(8,128)(2,1)} %get-tuple-element.10), calls=%async_computation | async-start | bytes 1048576 | tf_op jit(solution)/shard_map/all_to_all | solution.py:564
  53.7 0.0 copy-start
  53.7 0.0 copy-start.1
  53.7 0.0 copy-start.2
  53.7 6.2 %relay.1.foot_any = bf16[32,256,256]{2,1,0:T(8,128)(2,1)} custom-call(bf16[256,64,128]{2,1,0:T(8,128)(2,1)} %foot_any.1, f32[8,128]{1,0:T(8,128)} %get-tuple-element.11.after_ref), custom_call_target="tpu_custom_call" | custom-call | flops 20000000 | bytes 12000000 | tf_op jit(solution)/shard_map/relay/pallas_call | solution.py:420
  59.9 3.2 %all-to-all-done = bf16[8,4,64,128]{3,2,1,0:T(8,128)(2,1)S(1)} async-done(((bf16[8,4,64,128]{3,2,1,0:T(8,128)(2,1)}), bf16[8,4,64,128]{3,2,1,0:T(8,128)(2,1)S(1)}, u32[]{:S(2)}, u32[]{:S(2)}) %all-to-all-start) | async-done | bytes 524320 | tf_op jit(solution)/shard_map/all_to_all | solution.py:564
  63.0 0.0 copy-done
  63.1 0.0 copy-done.1
  63.1 0.0 copy-done.2
  63.1 4.5 %trace.1 = (bf16[32,64,128]{2,1,0:T(8,128)(2,1)}, bf16[512,34]{1,0:T(8,128)(2,1)S(1)}) custom-call(bf16[32,64,128]{2,1,0:T(8,128)(2,1)S(1)} %bitcast.12, f32[9]{0:T(128)S(1)} %copy-done.2, bf16[32,256,256]{2,1,0:T(8,128)(2,1)} %relay.1.foot_any, s32[1,256]{1,0:T(1,128)S(1)} %bitcast.14, s32[1,256]{1,0:T(1,128)S(1)} %bitcast.15), custom_call_target="tpu_custom_call" | custom-call | tf_op jit(solution)/shard_map/trace/pallas_call | solution.py:499
  67.6 19.2 %all_to_all.10 = bf16[128,4,34]{2,1,0:T(4,128)(2,1)} all-to-all(bf16[128,4,34]{2,1,0:T(4,128)(2,1)S(1)} %bitcast.13), channel_id=1, replica_groups=mesh['tm'=8,'tile'=16] {'tm','tile'}, dimensions={0} | all-to-all | bytes 69632 | tf_op jit(solution)/shard_map/all_to_all | solution.py:569
  86.8 1.9 %gather.1 = f32[32,320]{1,0:T(8,128)} custom-call(bf16[512,34]{1,0:T(8,128)(2,1)} %bitcast.17), custom_call_target="tpu_custom_call" | custom-call | tf_op jit(solution)/shard_map/gather/pallas_call | solution.py:528
  (2 shorter events, 0.1 us)
Async XLA Ops:
  1.5 9.2 %collective-permute-start = (bf16[4,3,1024]{2,1,0:T(4,128)(2,1)S(1)}, bf16[4,3,1024]{2,1,0:T(4,128)(2,1)S(1)}, u32[]{:S(2)}, u32[]{:S(2)}) collective-permute-start(bf16[4,3,1024]{2,1,0:T(4,128)(2,1)S(1)} %get-tuple-element.14), channel_id=1, source_target_pairs={{0,1},{1,2},{2,3},{3,4},{4,5},{5,6},{6,7},{7,8},{8,9},{9,10},{10,1... | collective-permute-start | bytes 73736 | tf_op jit(solution)/shard_map/ppermute | solution.py:554
  5.9 4.8 %collective-permute-start.1 = (bf16[4,3,1024]{2,1,0:T(4,128)(2,1)S(1)}, bf16[4,3,1024]{2,1,0:T(4,128)(2,1)S(1)}, u32[]{:S(2)}, u32[]{:S(2)}) collective-permute-start(bf16[4,3,1024]{2,1,0:T(4,128)(2,1)S(1)} %get-tuple-element.15), channel_id=1, source_target_pairs={{1,0},{2,1},{3,2},{4,3},{5,4},{6,5},{7,6},{8,7},{9,8},{10,9},{11,1... | collective-permute-start | bytes 73736 | tf_op jit(solution)/shard_map/ppermute | solution.py:555
  47.3 15.7 %all-to-all-start = ((bf16[8,4,64,128]{3,2,1,0:T(8,128)(2,1)}), bf16[8,4,64,128]{3,2,1,0:T(8,128)(2,1)S(1)}, u32[]{:S(2)}, u32[]{:S(2)}) async-start(bf16[8,4,64,128]{3,2,1,0:T(8,128)(2,1)} %get-tuple-element.10), calls=%async_computation | async-start | bytes 1048576 | tf_op jit(solution)/shard_map/all_to_all | solution.py:564
  53.7 9.4 %copy-start = (s32[256,1]{0,1:T(1,128)S(1)}, s32[256,1]{0,1:T(1,128)}, u32[]{:S(2)}) copy-start(s32[256,1]{0,1:T(1,128)} %param.20) | copy-start | bytes 3076
  53.7 9.4 %copy-start.1 = (s32[256]{0:T(256)S(1)}, s32[256]{0:T(256)}, u32[]{:S(2)}) copy-start(s32[256]{0:T(256)} %param.21) | copy-start | bytes 3076
  53.7 9.4 %copy-start.2 = (f32[9]{0:T(128)S(1)}, f32[9]{0:T(128)}, u32[]{:S(2)}) copy-start(f32[9]{0:T(128)} %tk_ref.1) | copy-start | bytes 112
